TPU v7x, 256 devices: a whole 4x4x8 slice. The times are simulated.
256 devices in a mesh: rows: 128 (over y, z, x), rep: 2 (over core).
Axes of the slice: x: 4, y: 4, z: 8, core: 2. Of those that a mesh axis runs over, the one named last changes fastest.
Arguments:
- grad_out: bfloat16 [16384, 1024], P('rows'), may hold values from -8 to 8
- w_self: bfloat16 [1024, 1024], replicated, may hold values from -0.1875 to 0.1875
- w_neigh: bfloat16 [1024, 1024], replicated, may hold values from -0.1875 to 0.1875
- adj_tiles: bfloat16 [128, 64, 128, 128], P('rows'), may hold values from -0.109375 to 0.109375
- tile_index: int32 [128, 64], P('rows'), may hold values from 0 to 127, as said below
- tile_count: int32 [128], P('rows'), may hold values from 4 to 64, as said below
- prompt_ids: int32 [16384], P('rows'), may hold values from 0 to 15
Outputs:
- input_grad: bfloat16 [16384, 1024], P('rows')
- prompt_grad: float32 [16, 1024], replicated
Inputs may be any that keep to these rules, and one draw needn't show every extreme that they name: `tile_index`: each row holds 64 different tile numbers; only the first tile_count entries of a row are used. `tile_count`: some destination tile uses all 64 slots.
All inputs are finite; a program needn't handle non-finite values.
Results may differ from a plain program's by a relative error of at most 0.0041.
Values may be sent and summed in bfloat16 or wider, within the bound.
No kernel may reach another device: no remote copies, remote signals or barrier semaphores. Data moves between devices by JAX's collectives and lax.ppermute only.
A program may use at most 64 MiB of HBM per device.

v0:
```python
import jax
import jax.numpy as jnp
from jax import lax
from jax.experimental import pallas as pl
from jax.experimental.pallas import tpu as pltpu
from jax.sharding import PartitionSpec as P

PROMPTS = 16
NX, NY, NZ, NREP = 4, 4, 8, 2
GROUP = 4
NEAR, REST = 20, 12
EMPTY = 128
AXES = ("rows", "rep")
ANY = pl.BlockSpec(memory_space=pl.ANY)
VMEM = pl.BlockSpec(memory_space=pltpu.VMEM)
SMEM = pl.BlockSpec(memory_space=pltpu.SMEM)


def pairs_of(role, step):
    pairs = []
    for y in range(NY):
        for z in range(NZ):
            for x in range(NX):
                for rep in range(NREP):
                    tx, ty, tz, trep = x, y, z, rep
                    if role == "rep":
                        trep = 1 - rep
                    elif role == "z":
                        tz = (z + step) % NZ
                    elif (role == "u") == (rep == 0):
                        tx = (x + step) % NX
                    else:
                        ty = (y + step) % NY
                    source = ((y * NZ + z) * NX + x) * NREP + rep
                    target = ((ty * NZ + tz) * NX + tx) * NREP + trep
                    pairs.append((source, target))
    return pairs


def send(value, role, step):
    return lax.ppermute(value, AXES, pairs_of(role, step))


def dot(a, b):
    return jnp.dot(a, b, preferred_element_type=jnp.float32)


def place():
    row, rep = lax.axis_index("rows"), lax.axis_index("rep")
    x, y = lax.rem(row, NX), lax.div(row, NX * NZ)
    z = lax.rem(lax.div(row, NX), NZ)
    u = jnp.where(rep == 0, x, y)
    v = jnp.where(rep == 0, y, x)
    return rep, u, v, z


def pack_kernel(adj, out, tiles, packed, in_sem, out_sem):
    steps = in_sem.shape[0]
    per = 64 // steps
    loads = []
    for i in range(steps):
        part = pl.ds(i * per, per)
        loads.append(pltpu.make_async_copy(adj.at[part], tiles.at[part], in_sem.at[i]))
    for i in range(steps // 2):
        loads[i].start()
        loads[steps // 2 + i].start()
    first = lax.broadcasted_iota(jnp.int32, (128, 128), 1) < 64
    rep = place()[0]
    stores = []
    for i in range(steps // 2):
        loads[i].wait()
        loads[steps // 2 + i].wait()

        @pl.when(rep == 0)
        def _():
            for k in range(i * per, i * per + per):
                packed[k] = jnp.where(first, tiles[k], pltpu.roll(tiles[32 + k], 64, 1))

        @pl.when(rep == 1)
        def _():
            for k in range(i * per, i * per + per):
                packed[k] = jnp.where(first, pltpu.roll(tiles[k], 64, 1), tiles[32 + k])

        part = pl.ds(i * per, per)
        stores.append(pltpu.make_async_copy(packed.at[part], out.at[part], out_sem.at[i]))
        stores[i].start()
    for store in stores:
        store.wait()


def pack(adj):
    return pl.pallas_call(
        pack_kernel,
        in_specs=[ANY],
        out_specs=ANY,
        out_shape=jax.ShapeDtypeStruct((32, 128, 128), jnp.bfloat16),
        scratch_shapes=[
            pltpu.VMEM((64, 128, 128), jnp.bfloat16),
            pltpu.VMEM((32, 128, 128), jnp.bfloat16),
            pltpu.SemaphoreType.DMA((8,)),
            pltpu.SemaphoreType.DMA((4,)),
        ],
        compiler_params=pltpu.CompilerParams(vmem_limit_bytes=16 * 2**20),
        name="pack",
    )(adj)


def split_kernel(count, index, ids, grad, *outs):
    rep, u, _, _ = place()
    start = pl.multiple_of(rep * 64, 64)
    as_rows = lambda value: jnp.broadcast_to(value.astype(jnp.float32), (16, value.shape[1]))
    sources = as_rows(index[...]).astype(jnp.bfloat16)
    numbers = as_rows(ids[...]).astype(jnp.bfloat16)
    used = jnp.full((16, 64), count[0].astype(jnp.float32)).astype(jnp.bfloat16)
    for step in range(GROUP):
        outs[step][0:64, :] = grad[pl.ds(start, 64), lanes_of(u, step)]
        outs[step][64:80, 0:64] = sources
        outs[step][64:80, 64:128] = used
        outs[step][64:80, 128:256] = numbers


def split(count, index, ids, grad):
    shape = jax.ShapeDtypeStruct((80, 256), jnp.bfloat16)
    return pl.pallas_call(
        split_kernel,
        in_specs=[SMEM, VMEM, VMEM, VMEM],
        out_specs=[VMEM] * GROUP,
        out_shape=[shape] * GROUP,
        name="split",
    )(count, index, ids, grad)


def unpack_kernel(*refs):
    packed, (own, where, ids) = refs[0:GROUP], refs[GROUP:]
    rep, u, v, z = place()
    rows = []
    for s in range(GROUP):
        own[64 * s : 64 * s + 64, :] = packed[s][0:64, :]
        rows.append(packed[s][64:80, :].astype(jnp.float32)[0:1])
    rows = jnp.concatenate(rows, axis=0).astype(jnp.int32)
    ids[...] = rows[:, 128:256]
    source = rows[:, 0:128]
    sx, sz, sy = source & (NX - 1), (source >> 2) & (NZ - 1), source >> 5
    du = (u - jnp.where(rep == 0, sx, sy)) & (GROUP - 1)
    dv = (v - jnp.where(rep == 0, sy, sx)) & (GROUP - 1)
    dz = (z - sz) & (NZ - 1)
    spot = jnp.zeros_like(dz)
    for i, p in enumerate((0, 1, 3, 5, 6, 7, 4, 2)):
        spot = jnp.where(dz == i, p, spot)
    lane = lax.broadcasted_iota(jnp.int32, (GROUP, 128), 1)
    count = jnp.max(jnp.where(lane == 64, source, 0), axis=1, keepdims=True)
    where[...] = jnp.where(lane < count, dv * 32 + spot * 4 + du, EMPTY)


def unpack(packed):
    return pl.pallas_call(
        unpack_kernel,
        in_specs=[VMEM] * GROUP,
        out_specs=[VMEM] * 3,
        out_shape=[
            jax.ShapeDtypeStruct((256, 256), jnp.bfloat16),
            jax.ShapeDtypeStruct((GROUP, 128), jnp.int32),
            jax.ShapeDtypeStruct((GROUP, 128), jnp.int32),
        ],
        name="unpack",
    )(*packed)


def join_kernel(*refs):
    pieces, out = refs[:-1], refs[-1]
    for i, piece in enumerate(pieces):
        out[256 * i : 256 * i + 256, :] = piece[...]


def join(*pieces):
    return pl.pallas_call(
        join_kernel,
        in_specs=[VMEM] * len(pieces),
        out_specs=VMEM,
        out_shape=jax.ShapeDtypeStruct((256 * len(pieces), 256), jnp.bfloat16),
        name="join",
    )(*pieces)


def aggregate_kernel(where, ids, *refs):
    tiles = refs[0:5]
    chunks = refs[5:13]
    parts = refs[13:17]
    sums = refs[17]
    adj, table, adj_sem, table_sem = refs[18:]
    table_copies, adj_copies = [], []
    for i in range(8):
        length = NEAR if i % 2 == 0 else REST
        begin = i // 2 * 32 + (0 if i % 2 == 0 else NEAR)
        copy = pltpu.make_async_copy(
            chunks[i], table.at[pl.ds(begin, length)], table_sem.at[i]
        )
        copy.start()
        table_copies.append(copy)
    begin = 0
    for i in range(5):
        length = tiles[i].shape[0]
        copy = pltpu.make_async_copy(tiles[i], adj.at[pl.ds(begin, length)], adj_sem.at[i])
        copy.start()
        adj_copies.append(copy)
        begin += length
    table[EMPTY] = jnp.zeros((64, 256), jnp.bfloat16)
    for copy in table_copies:
        copy.wait()
    total = jnp.zeros((PROMPTS, 256), jnp.float32)
    own = jnp.zeros((PROMPTS, 256), jnp.float32)
    rep = place()[0]
    for d in range(GROUP):
        for i in ((0,), (1,), (2, 3), (4,))[d]:
            adj_copies[i].wait()
        acc = jnp.zeros((128, 256), jnp.float32)
        for q in range(16):
            p = 2 * q
            left = jnp.concatenate([adj[d * 32 + p], adj[d * 32 + p + 1]], axis=1)
            rows = [table[where[d, k]] for k in (p, p + 32, p + 1, p + 33)]
            acc = acc + dot(left, jnp.concatenate(rows, axis=0))
        parts[d][...] = acc
        number = lax.broadcasted_iota(jnp.int32, (PROMPTS, 128), 0)
        hot = jnp.where(ids[d : d + 1, :] == number, 1.0, 0.0).astype(jnp.bfloat16)
        high = acc.astype(jnp.bfloat16)
        low = (acc - high.astype(jnp.float32)).astype(jnp.bfloat16)
        total = total + dot(hot, high) + dot(hot, low)
        row = lax.broadcasted_iota(jnp.int32, (128, 1), 0)
        mine = (row // 64) == rep
        block = jnp.concatenate([table[d], table[d]], axis=0)
        block = jnp.where(mine, block.astype(jnp.float32), 0.0).astype(jnp.bfloat16)
        own = own + dot(hot, block)
    sums[0:PROMPTS, :] = own
    sums[PROMPTS : 2 * PROMPTS, :] = total


def aggregate(where, ids, tiles, chunks):
    part = jax.ShapeDtypeStruct((128, 256), jnp.float32)
    return pl.pallas_call(
        aggregate_kernel,
        in_specs=[SMEM, VMEM] + [ANY] * 13,
        out_specs=[VMEM] * 5,
        out_shape=[part] * 4 + [jax.ShapeDtypeStruct((2 * PROMPTS, 256), jnp.float32)],
        scratch_shapes=[
            pltpu.VMEM((128, 128, 128), jnp.bfloat16),
            pltpu.VMEM((EMPTY + 1, 64, 256), jnp.bfloat16),
            pltpu.SemaphoreType.DMA((5,)),
            pltpu.SemaphoreType.DMA((8,)),
        ],
        compiler_params=pltpu.CompilerParams(vmem_limit_bytes=24 * 2**20),
        name="aggregate",
    )(where, ids, *tiles, *chunks)


def lanes_of(u, step):
    piece = lax.rem(u + step, GROUP)
    return pl.ds(pl.multiple_of(piece * 256, 256), 256)


ORDER = (0, 1, 3, 2)


def gather_pieces(groups, total, sem):
    _, u, v, _ = place()
    copies = []
    for j, pieces in enumerate(groups):
        for i, step in enumerate(ORDER):
            target = total.at[j, :, lanes_of((u, v)[j], step)]
            copies.append(pltpu.make_async_copy(pieces[i], target, sem.at[j, i]))
    for copy in copies:
        copy.start()
    for copy in copies:
        copy.wait()


def dot_t(a, b):
    return lax.dot_general(a, b, (((1,), (1,)), ((), ())), preferred_element_type=jnp.float32)


def finish_kernel(self_term, weight, *refs):
    mine, other, out, total, sem = refs[0:4], refs[4:8], refs[8], refs[9], refs[10]
    gather_pieces((mine, other), total, sem)
    neighbours = (total[0] + total[1]).astype(jnp.bfloat16)
    out[...] = (self_term[...] + dot_t(neighbours, weight[...])).astype(jnp.bfloat16)


def finish(self_term, weight, mine, other):
    return pl.pallas_call(
        finish_kernel,
        in_specs=[VMEM] * 2 + [ANY] * 8,
        out_specs=VMEM,
        out_shape=jax.ShapeDtypeStruct((128, 1024), jnp.bfloat16),
        scratch_shapes=[
            pltpu.VMEM((2, 128, 1024), jnp.float32),
            pltpu.SemaphoreType.DMA((2, GROUP)),
        ],
        compiler_params=pltpu.CompilerParams(vmem_limit_bytes=24 * 2**20),
        name="finish",
    )(self_term, weight, *mine, *other)


def dot_wide(a, b):
    high = a.astype(jnp.bfloat16)
    rest = a - high.astype(jnp.float32)
    middle = rest.astype(jnp.bfloat16)
    low = (rest - middle.astype(jnp.float32)).astype(jnp.bfloat16)
    product = dot_t(jnp.concatenate([high, middle, low], axis=0), b)
    return product[0:16] + product[16:32] + product[32:48]


def prompt_kernel(weight_self, weight_neigh, *refs):
    mine, out, total, sem = refs[0:4], refs[4], refs[5], refs[6]
    gather_pieces((mine,), total, sem)
    sums = total[0]
    first = dot_wide(sums[0:16, :], weight_self[...])
    out[...] = first + dot_wide(sums[16:32, :], weight_neigh[...])


def prompt(weight_self, weight_neigh, mine):
    return pl.pallas_call(
        prompt_kernel,
        in_specs=[VMEM] * 2 + [ANY] * 4,
        out_specs=VMEM,
        out_shape=jax.ShapeDtypeStruct((PROMPTS, 1024), jnp.float32),
        scratch_shapes=[
            pltpu.VMEM((1, 2 * PROMPTS, 1024), jnp.float32),
            pltpu.SemaphoreType.DMA((1, GROUP)),
        ],
        compiler_params=pltpu.CompilerParams(vmem_limit_bytes=24 * 2**20),
        name="prompt",
    )(weight_self, weight_neigh, *mine)


def total_of_four(value, role):
    near = send(value, role, 1), send(value, role, -1)
    return (value + send(value, role, 2)) + (near[0] + near[1])


def shards(grad_out, w_self, w_neigh, adj_tiles, tile_index, tile_count, prompt_ids):
    shares = split(tile_count, tile_index, prompt_ids[None, :], grad_out)
    packed = [shares[0]] + [send(shares[s], "u", s) for s in range(1, GROUP)]
    mine = pack(adj_tiles[0])
    mine, packed = lax.optimization_barrier((mine, packed))
    own, where, ids = unpack(packed)
    left, right = send(mine, "u", 1), send(mine, "u", -1)

    z1, z7, z2, z6 = [send(own, "z", s) for s in (1, -1, 2, -2)]
    z3, z4, z5 = send(z2, "z", 1), send(z2, "z", 2), send(z6, "z", -1)

    near = join(own, z1, z7, z2, z6)
    near_m, near_p = send(near, "v", 1), send(near, "v", -1)
    far = [send(left[0:16], "u", 1), send(right[16:32], "u", -1)]
    tiles = [mine, left, *far, right]
    rest = join(z3, z4, z5)
    self_term, rest = lax.optimization_barrier((dot_t(grad_out, w_self), rest))
    rest_m, rest_p = send(rest, "v", 1), send(rest, "v", -1)
    near_2, rest_2 = send(near_m, "v", 1), send(rest_p, "v", -1)
    chunks = [near, rest, near_m, rest_m, near_2, rest_2, near_p, rest_p]
    chunks = [c.reshape(c.shape[0] // 64, 64, 256) for c in chunks]

    *parts, sums = aggregate(where, ids, tiles, chunks)

    owned = [
        parts[0],
        send(parts[1], "u", -1),
        send(parts[3], "u", 1),
        send(parts[2], "u", 2),
    ]

    sums = total_of_four(sums, "v")
    sums = sums + send(sums, "z", 4)
    sums = total_of_four(sums, "z")
    pieces = [sums, send(sums, "u", -1), send(sums, "u", 1), send(sums, "u", 2)]
    owned, pieces = lax.optimization_barrier((owned, pieces))
    product = prompt(w_self, w_neigh, pieces)
    prompt_grad = product + send(product, "rep", 0)
    other = [send(m, "rep", 0) for m in owned]
    input_grad = finish(self_term, w_neigh, owned, other)
    return input_grad, prompt_grad


def solution(mesh):
    placed = (
        P("rows", None),
        P(),
        P(),
        P("rows", None, None, None),
        P("rows", None),
        P("rows"),
        P("rows"),
    )
    return jax.shard_map(
        shards, mesh=mesh, in_specs=placed, out_specs=(P("rows", None), P()), check_vma=False
    )
```

profile of v0, /device:TPU:1, one launch (start us, length us, event | category | flops | bytes accessed | tf_op | source)
XLA Modules:
  0.0 122.7 jit_solution(1849189455790463363)
XLA Ops:
  1.3 1.7 %split.1 = (bf16[80,256]{1,0:T(8,128)(2,1)}, bf16[80,256]{1,0:T(8,128)(2,1)}, bf16[80,256]{1,0:T(8,128)(2,1)}, bf16[80,256]{1,0:T(8,128)(2,1)}) custom-call(s32[1]{0:T(128)S(6)} %copy.9.count, s32[1,64]{1,0:T(1,128)} %index.1, s32[1,128]{1,0:T(1,128)} %bitcast.20, bf16[128,1024]{1,0:T(8,128)(2,1)} %grad.1), custom_call_target="tpu_custom_call" | custom-call | tf_op jit(solution)/shard_map/split/pallas_call | solution.py:124
  2.9 2.1 %collective-permute-start = (bf16[80,256]{1,0:T(8,128)(2,1)}, bf16[80,256]{1,0:T(8,128)(2,1)S(1)}, u32[]{:S(2)}, u32[]{:S(2)}) collective-permute-start(bf16[80,256]{1,0:T(8,128)(2,1)} %get-tuple-element.30), channel_id=1, source_target_pairs={{0,2},{1,65},{2,4},{3,67},{4,6},{5,69},{6,0},{7,71},{8,10},{9,73},... | collective-permute-start | bytes 122888 | tf_op jit(solution)/shard_map/ppermute | solution.py:41
  5.1 2.6 %collective-permute-start.1 = (bf16[80,256]{1,0:T(8,128)(2,1)}, bf16[80,256]{1,0:T(8,128)(2,1)S(1)}, u32[]{:S(2)}, u32[]{:S(2)}) collective-permute-start(bf16[80,256]{1,0:T(8,128)(2,1)} %get-tuple-element.31), channel_id=1, source_target_pairs={{0,4},{1,129},{2,6},{3,131},{4,0},{5,133},{6,2},{7,135},{8,12},{9,... | collective-permute-start | bytes 122888 | tf_op jit(solution)/shard_map/ppermute | solution.py:41
  8.8 1.6 %copy-done.3 = bf16[1,64,128,128]{3,2,1,0:T(8,128)(2,1)S(1)} copy-done((bf16[1,64,128,128]{3,2,1,0:T(8,128)(2,1)S(1)}, bf16[1,64,128,128]{3,2,1,0:T(8,128)(2,1)}, u32[]{:S(2)}) %copy-start.3) | copy-done | bytes 2097176
  11.3 1.7 %collective-permute-start.10 = (bf16[32,128,128]{2,1,0:T(8,128)(2,1)S(1)}, bf16[32,128,128]{2,1,0:T(8,128)(2,1)}, u32[]{:S(2)}, u32[]{:S(2)}) collective-permute-start(bf16[32,128,128]{2,1,0:T(8,128)(2,1)S(1)} %pack.1.refs_0_), channel_id=1, source_target_pairs={{0,6},{1,193},{2,0},{3,195},{4,2},{5,197},{6,4},{7,199},{8,14},{9,... | collective-permute-start | bytes 3145736 | tf_op jit(solution)/shard_map/ppermute | solution.py:41
  13.0 1.6 %unpack.1 = (bf16[256,256]{1,0:T(8,128)(2,1)}, s32[4,128]{1,0:T(4,128)}, s32[4,128]{1,0:T(4,128)}) custom-call(bf16[80,256]{1,0:T(8,128)(2,1)} %get-tuple-element.33.refs_0_, bf16[80,256]{1,0:T(8,128)(2,1)} %copy-done.13, bf16[80,256]{1,0:T(8,128)(2,1)} %copy-done.14, bf16[80,256]{1,0:T(8,128)(2,1)} %copy-done.15), custom_call_target="tpu_custom_call" | custom-call | tf_op jit(solution)/shard_map/unpack/pallas_call | solution.py:156
  14.6 5.6 %collective-permute-start.13 = (bf16[256,256]{1,0:T(8,128)(2,1)}, bf16[256,256]{1,0:T(8,128)(2,1)S(1)}, u32[]{:S(2)}, u32[]{:S(2)}) collective-permute-start(bf16[256,256]{1,0:T(8,128)(2,1)} %get-tuple-element.37.refs_0_), channel_id=1, source_target_pairs={{0,56},{1,57},{2,58},{3,59},{4,60},{5,61},{6,62},{7,63},{8,0},{9,1... | collective-permute-start | bytes 393224 | tf_op jit(solution)/shard_map/ppermute | solution.py:41
  22.7 3.6 %collective-permute-done.6.refs_4_ = bf16[256,256]{1,0:T(8,128)(2,1)} collective-permute-done((bf16[256,256]{1,0:T(8,128)(2,1)}, bf16[256,256]{1,0:T(8,128)(2,1)}, u32[]{:S(2)}, u32[]{:S(2)}) %collective-permute-start.6) | collective-permute-done | bytes 131104 | tf_op jit(solution)/shard_map/ppermute | solution.py:41
  26.3 2.3 %collective-permute-start.7 = (bf16[256,256]{1,0:T(8,128)(2,1)}, bf16[256,256]{1,0:T(8,128)(2,1)}, u32[]{:S(2)}, u32[]{:S(2)}) collective-permute-start(bf16[256,256]{1,0:T(8,128)(2,1)} %collective-permute-done.6.refs_4_), channel_id=1, source_target_pairs={{0,56},{1,57},{2,58},{3,59},{4,60},{5,61},{6,62},{7,63},{8,0},{9,1... | collective-permute-start | bytes 393224 | tf_op jit(solution)/shard_map/ppermute | solution.py:41
  30.1 2.0 %join.3 = bf16[1280,256]{1,0:T(8,128)(2,1)} custom-call(bf16[256,256]{1,0:T(8,128)(2,1)} %get-tuple-element.37.refs_0_, bf16[256,256]{1,0:T(8,128)(2,1)} %copy-done.11, bf16[256,256]{1,0:T(8,128)(2,1)} %copy-done.10, bf16[256,256]{1,0:T(8,128)(2,1)} %copy-done.9, bf16[256,256]{1,0:T(8,128)(2,1)} %collective-permute-done.6.refs_4_), custom_call_target="tpu_custom_call" | custom-call | tf_op jit(solution)/shard_map/join/pallas_call | solution.py:176
  33.4 2.4 %collective-permute-start.5 = (bf16[256,256]{1,0:T(8,128)(2,1)}, bf16[256,256]{1,0:T(8,128)(2,1)S(1)}, u32[]{:S(2)}, u32[]{:S(2)}) collective-permute-start(bf16[256,256]{1,0:T(8,128)(2,1)} %copy-done.9), channel_id=1, source_target_pairs={{0,16},{1,17},{2,18},{3,19},{4,20},{5,21},{6,22},{7,23},{8,24},{9,... | collective-permute-start | bytes 393224 | tf_op jit(solution)/shard_map/ppermute | solution.py:41
  35.8 2.0 %collective-permute-start.4 = (bf16[256,256]{1,0:T(8,128)(2,1)}, bf16[256,256]{1,0:T(8,128)(2,1)}, u32[]{:S(2)}, u32[]{:S(2)}) collective-permute-start(bf16[256,256]{1,0:T(8,128)(2,1)} %copy-done.9), channel_id=1, source_target_pairs={{0,8},{1,9},{2,10},{3,11},{4,12},{5,13},{6,14},{7,15},{8,16},{9,17... | collective-permute-start | bytes 393224 | tf_op jit(solution)/shard_map/ppermute | solution.py:41
  37.7 1.6 %fusion.self_term = f32[128,1024]{1,0:T(8,128)} fusion(bf16[128,1024]{1,0:T(8,128)(2,1)S(1)} %copy-done.8, bf16[1024,1024]{1,0:T(8,128)(2,1)S(1)} %copy-done), kind=kOutput, calls=%fused_computation.2 | convolution fusion | flops 268435456 | bytes 2883584 | tf_op jit(solution)/shard_map/dot_general | solution.py:277
  40.1 3.2 %collective-permute-done.4.refs_0_ = bf16[256,256]{1,0:T(8,128)(2,1)} collective-permute-done((bf16[256,256]{1,0:T(8,128)(2,1)}, bf16[256,256]{1,0:T(8,128)(2,1)}, u32[]{:S(2)}, u32[]{:S(2)}) %collective-permute-start.4) | collective-permute-done | bytes 131104 | tf_op jit(solution)/shard_map/ppermute | solution.py:41
  43.3 1.8 %join.2 = bf16[768,256]{1,0:T(8,128)(2,1)} custom-call(bf16[256,256]{1,0:T(8,128)(2,1)} %collective-permute-done.4.refs_0_, bf16[256,256]{1,0:T(8,128)(2,1)} %copy-done.12, bf16[256,256]{1,0:T(8,128)(2,1)} %collective-permute-done.7.refs_2_), custom_call_target="tpu_custom_call" | custom-call | tf_op jit(solution)/shard_map/join/pallas_call | solution.py:176
  45.1 2.0 %collective-permute-start.17 = (bf16[768,256]{1,0:T(8,128)(2,1)}, bf16[768,256]{1,0:T(8,128)(2,1)S(1)}, u32[]{:S(2)}, u32[]{:S(2)}) collective-permute-start(bf16[768,256]{1,0:T(8,128)(2,1)} %join.2), channel_id=1, source_target_pairs={{0,192},{1,7},{2,194},{3,1},{4,196},{5,3},{6,198},{7,5},{8,200},{9... | collective-permute-start | bytes 1179656 | tf_op jit(solution)/shard_map/ppermute | solution.py:41
  47.2 7.5 %collective-permute-start.15 = (bf16[768,256]{1,0:T(8,128)(2,1)}, bf16[768,256]{1,0:T(8,128)(2,1)S(1)}, u32[]{:S(2)}, u32[]{:S(2)}) collective-permute-start(bf16[768,256]{1,0:T(8,128)(2,1)} %join.2), channel_id=1, source_target_pairs={{0,64},{1,3},{2,66},{3,5},{4,68},{5,7},{6,70},{7,1},{8,72},{9,11},... | collective-permute-start | bytes 1179656 | tf_op jit(solution)/shard_map/ppermute | solution.py:41
  58.4 1.9 %collective-permute-done.17 = bf16[768,256]{1,0:T(8,128)(2,1)S(1)} collective-permute-done((bf16[768,256]{1,0:T(8,128)(2,1)}, bf16[768,256]{1,0:T(8,128)(2,1)S(1)}, u32[]{:S(2)}, u32[]{:S(2)}) %collective-permute-start.17) | collective-permute-done | bytes 393248 | tf_op jit(solution)/shard_map/ppermute | solution.py:41
  60.3 2.1 %collective-permute-start.18 = (bf16[768,256]{1,0:T(8,128)(2,1)S(1)}, bf16[768,256]{1,0:T(8,128)(2,1)S(1)}, u32[]{:S(2)}, u32[]{:S(2)}) collective-permute-start(bf16[768,256]{1,0:T(8,128)(2,1)S(1)} %collective-permute-done.17), channel_id=1, source_target_pairs={{0,192},{1,7},{2,194},{3,1},{4,196},{5,3},{6,198},{7,5},{8,200},{9... | collective-permute-start | bytes 1179656 | tf_op jit(solution)/shard_map/ppermute | solution.py:41
  62.3 10.6 %collective-permute-done.19 = bf16[1280,256]{1,0:T(8,128)(2,1)S(1)} collective-permute-done((bf16[1280,256]{1,0:T(8,128)(2,1)}, bf16[1280,256]{1,0:T(8,128)(2,1)S(1)}, u32[]{:S(2)}, u32[]{:S(2)}) %collective-permute-start.19) | collective-permute-done | bytes 655392 | tf_op jit(solution)/shard_map/ppermute | solution.py:41
  72.9 3.9 %collective-permute-done.18 = bf16[768,256]{1,0:T(8,128)(2,1)S(1)} collective-permute-done((bf16[768,256]{1,0:T(8,128)(2,1)S(1)}, bf16[768,256]{1,0:T(8,128)(2,1)S(1)}, u32[]{:S(2)}, u32[]{:S(2)}) %collective-permute-start.18) | collective-permute-done | bytes 393248 | tf_op jit(solution)/shard_map/ppermute | solution.py:41
  76.9 5.6 %aggregate.1 = (f32[128,256]{1,0:T(8,128)S(1)}, f32[128,256]{1,0:T(8,128)S(1)}, f32[128,256]{1,0:T(8,128)S(1)}, f32[128,256]{1,0:T(8,128)S(1)}, f32[32,256]{1,0:T(8,128)S(1)}) custom-call(s32[4,128]{1,0:T(4,128)S(1)} %copy-done.6, s32[4,128]{1,0:T(4,128)S(1)} %copy-done.7, bf16[32,128,128]{2,1,0:T(8,128)(2,1)S(1)} %pack.1.refs_0_, ...), custom_call_target="tpu_custom_call" | custom-call | tf_op jit(solution)/shard_map/aggregate/pallas_call | solution.py:239
  82.6 1.8 %collective-permute-start.24 = (f32[32,256]{1,0:T(8,128)S(1)}, f32[32,256]{1,0:T(8,128)S(1)}, u32[]{:S(2)}, u32[]{:S(2)}) collective-permute-start(f32[32,256]{1,0:T(8,128)S(1)} %get-tuple-element.47), channel_id=1, source_target_pairs={{0,64},{1,3},{2,66},{3,5},{4,68},{5,7},{6,70},{7,1},{8,72},{9,11},... | collective-permute-start | bytes 98312 | tf_op jit(solution)/shard_map/ppermute | solution.py:41
  84.4 1.7 %collective-permute-start.23 = (f32[32,256]{1,0:T(8,128)S(1)}, f32[32,256]{1,0:T(8,128)S(1)}, u32[]{:S(2)}, u32[]{:S(2)}) collective-permute-start(f32[32,256]{1,0:T(8,128)S(1)} %get-tuple-element.47), channel_id=1, source_target_pairs={{0,128},{1,5},{2,130},{3,7},{4,132},{5,1},{6,134},{7,3},{8,136},{9... | collective-permute-start | bytes 98312 | tf_op jit(solution)/shard_map/ppermute | solution.py:41
  86.6 2.0 %collective-permute-done.23 = f32[32,256]{1,0:T(8,128)S(1)} collective-permute-done((f32[32,256]{1,0:T(8,128)S(1)}, f32[32,256]{1,0:T(8,128)S(1)}, u32[]{:S(2)}, u32[]{:S(2)}) %collective-permute-start.23) | collective-permute-done | bytes 32800 | tf_op jit(solution)/shard_map/ppermute | solution.py:41
  89.3 6.2 %collective-permute-done.26 = f32[32,256]{1,0:T(8,128)S(1)} collective-permute-done((f32[32,256]{1,0:T(8,128)S(1)}, f32[32,256]{1,0:T(8,128)S(1)}, u32[]{:S(2)}, u32[]{:S(2)}) %collective-permute-start.26) | collective-permute-done | bytes 32800 | tf_op jit(solution)/shard_map/ppermute | solution.py:41
  97.0 1.5 %collective-permute-start.21 = (f32[128,256]{1,0:T(8,128)S(1)}, f32[128,256]{1,0:T(8,128)S(1)}, u32[]{:S(2)}, u32[]{:S(2)}) collective-permute-start(f32[128,256]{1,0:T(8,128)S(1)} %get-tuple-element.45), channel_id=1, source_target_pairs={{0,2},{1,65},{2,4},{3,67},{4,6},{5,69},{6,0},{7,71},{8,10},{9,73},... | collective-permute-start | bytes 393224 | tf_op jit(solution)/shard_map/ppermute | solution.py:41
  99.6 2.4 %collective-permute-done.27 = f32[32,256]{1,0:T(8,128)S(1)} collective-permute-done((f32[32,256]{1,0:T(8,128)S(1)}, f32[32,256]{1,0:T(8,128)S(1)}, u32[]{:S(2)}, u32[]{:S(2)}) %collective-permute-start.27) | collective-permute-done | bytes 32800 | tf_op jit(solution)/shard_map/ppermute | solution.py:41
  102.2 4.4 %collective-permute-done.32.refs_3_ = f32[32,256]{1,0:T(8,128)S(1)} collective-permute-done((f32[32,256]{1,0:T(8,128)S(1)}, f32[32,256]{1,0:T(8,128)S(1)}, u32[]{:S(2)}, u32[]{:S(2)}) %collective-permute-start.32) | collective-permute-done | bytes 32800 | tf_op jit(solution)/shard_map/ppermute | solution.py:41
  106.6 3.1 %collective-permute-done.30.refs_1_ = f32[32,256]{1,0:T(8,128)S(1)} collective-permute-done((f32[32,256]{1,0:T(8,128)S(1)}, f32[32,256]{1,0:T(8,128)S(1)}, u32[]{:S(2)}, u32[]{:S(2)}) %collective-permute-start.30) | collective-permute-done | bytes 32800 | tf_op jit(solution)/shard_map/ppermute | solution.py:41
  109.7 7.0 %collective-permute-start.33 = (f32[128,256]{1,0:T(8,128)S(1)}, f32[128,256]{1,0:T(8,128)S(1)}, u32[]{:S(2)}, u32[]{:S(2)}) collective-permute-start(f32[128,256]{1,0:T(8,128)S(1)} %get-tuple-element.48.refs_0_), channel_id=1, source_target_pairs={{0,1},{1,0},{2,3},{3,2},{4,5},{5,4},{6,7},{7,6},{8,9},{9,8},{10,11... | collective-permute-start | bytes 393224 | tf_op jit(solution)/shard_map/ppermute | solution.py:41
  120.8 1.8 %finish.1 = bf16[128,1024]{1,0:T(8,128)(2,1)} custom-call(f32[128,1024]{1,0:T(8,128)S(1)} %copy-done.4, bf16[1024,1024]{1,0:T(8,128)(2,1)S(1)} %copy-done.1, f32[128,256]{1,0:T(8,128)S(1)} %get-tuple-element.48.refs_0_, f32[128,256]{1,0:T(8,128)S(1)} %collective-permute-done.20.refs_1_, f32[128,256]{1,0:T(8,128)S(1)} %collective-permute-done.21.refs_2_, ...), custom_call_target="tpu_custom_call" | custom-call | tf_op jit(solution)/shard_map/finish/pallas_call | solution.py:288
  (91 shorter events, 19.8 us)
Async XLA Ops:
  2.9 8.3 %collective-permute-start = (bf16[80,256]{1,0:T(8,128)(2,1)}, bf16[80,256]{1,0:T(8,128)(2,1)S(1)}, u32[]{:S(2)}, u32[]{:S(2)}) collective-permute-start(bf16[80,256]{1,0:T(8,128)(2,1)} %get-tuple-element.30), channel_id=1, source_target_pairs={{0,2},{1,65},{2,4},{3,67},{4,6},{5,69},{6,0},{7,71},{8,10},{9,73},... | collective-permute-start | bytes 122888 | tf_op jit(solution)/shard_map/ppermute | solution.py:41
  5.1 6.2 %collective-permute-start.1 = (bf16[80,256]{1,0:T(8,128)(2,1)}, bf16[80,256]{1,0:T(8,128)(2,1)S(1)}, u32[]{:S(2)}, u32[]{:S(2)}) collective-permute-start(bf16[80,256]{1,0:T(8,128)(2,1)} %get-tuple-element.31), channel_id=1, source_target_pairs={{0,4},{1,129},{2,6},{3,131},{4,0},{5,133},{6,2},{7,135},{8,12},{9,... | collective-permute-start | bytes 122888 | tf_op jit(solution)/shard_map/ppermute | solution.py:41
  11.3 43.3 %collective-permute-start.10 = (bf16[32,128,128]{2,1,0:T(8,128)(2,1)S(1)}, bf16[32,128,128]{2,1,0:T(8,128)(2,1)}, u32[]{:S(2)}, u32[]{:S(2)}) collective-permute-start(bf16[32,128,128]{2,1,0:T(8,128)(2,1)S(1)} %pack.1.refs_0_), channel_id=1, source_target_pairs={{0,6},{1,193},{2,0},{3,195},{4,2},{5,197},{6,4},{7,199},{8,14},{9,... | collective-permute-start | bytes 3145736 | tf_op jit(solution)/shard_map/ppermute | solution.py:41
  14.6 7.8 %collective-permute-start.13 = (bf16[256,256]{1,0:T(8,128)(2,1)}, bf16[256,256]{1,0:T(8,128)(2,1)S(1)}, u32[]{:S(2)}, u32[]{:S(2)}) collective-permute-start(bf16[256,256]{1,0:T(8,128)(2,1)} %get-tuple-element.37.refs_0_), channel_id=1, source_target_pairs={{0,56},{1,57},{2,58},{3,59},{4,60},{5,61},{6,62},{7,63},{8,0},{9,1... | collective-permute-start | bytes 393224 | tf_op jit(solution)/shard_map/ppermute | solution.py:41
  20.2 37.0 %collective-permute-start.8 = (bf16[32,128,128]{2,1,0:T(8,128)(2,1)S(1)}, bf16[32,128,128]{2,1,0:T(8,128)(2,1)}, u32[]{:S(2)}, u32[]{:S(2)}) collective-permute-start(bf16[32,128,128]{2,1,0:T(8,128)(2,1)S(1)} %pack.1.refs_0_), channel_id=1, source_target_pairs={{0,2},{1,65},{2,4},{3,67},{4,6},{5,69},{6,0},{7,71},{8,10},{9,73},... | collective-permute-start | bytes 3145736 | tf_op jit(solution)/shard_map/ppermute | solution.py:41
  20.2 6.1 %collective-permute-start.6 = (bf16[256,256]{1,0:T(8,128)(2,1)}, bf16[256,256]{1,0:T(8,128)(2,1)}, u32[]{:S(2)}, u32[]{:S(2)}) collective-permute-start(bf16[256,256]{1,0:T(8,128)(2,1)} %get-tuple-element.37.refs_0_), channel_id=1, source_target_pairs={{0,48},{1,49},{2,50},{3,51},{4,52},{5,53},{6,54},{7,55},{8,56},{9,... | collective-permute-start | bytes 393224 | tf_op jit(solution)/shard_map/ppermute | solution.py:41
  21.4 7.2 %collective-permute-start.12 = (bf16[256,256]{1,0:T(8,128)(2,1)}, bf16[256,256]{1,0:T(8,128)(2,1)S(1)}, u32[]{:S(2)}, u32[]{:S(2)}) collective-permute-start(bf16[256,256]{1,0:T(8,128)(2,1)} %get-tuple-element.37.refs_0_), channel_id=1, source_target_pairs={{0,8},{1,9},{2,10},{3,11},{4,12},{5,13},{6,14},{7,15},{8,16},{9,17... | collective-permute-start | bytes 393224 | tf_op jit(solution)/shard_map/ppermute | solution.py:41
  22.5 7.0 %collective-permute-start.3 = (bf16[256,256]{1,0:T(8,128)(2,1)}, bf16[256,256]{1,0:T(8,128)(2,1)S(1)}, u32[]{:S(2)}, u32[]{:S(2)}) collective-permute-start(bf16[256,256]{1,0:T(8,128)(2,1)} %get-tuple-element.37.refs_0_), channel_id=1, source_target_pairs={{0,16},{1,17},{2,18},{3,19},{4,20},{5,21},{6,22},{7,23},{8,24},{9,... | collective-permute-start | bytes 393224 | tf_op jit(solution)/shard_map/ppermute | solution.py:41
  26.3 9.5 %collective-permute-start.7 = (bf16[256,256]{1,0:T(8,128)(2,1)}, bf16[256,256]{1,0:T(8,128)(2,1)}, u32[]{:S(2)}, u32[]{:S(2)}) collective-permute-start(bf16[256,256]{1,0:T(8,128)(2,1)} %collective-permute-done.6.refs_4_), channel_id=1, source_target_pairs={{0,56},{1,57},{2,58},{3,59},{4,60},{5,61},{6,62},{7,63},{8,0},{9,1... | collective-permute-start | bytes 393224 | tf_op jit(solution)/shard_map/ppermute | solution.py:41
  32.1 22.5 %collective-permute-start.14 = (bf16[1280,256]{1,0:T(8,128)(2,1)}, bf16[1280,256]{1,0:T(8,128)(2,1)}, u32[]{:S(2)}, u32[]{:S(2)}) collective-permute-start(bf16[1280,256]{1,0:T(8,128)(2,1)} %join.3), channel_id=1, source_target_pairs={{0,64},{1,3},{2,66},{3,5},{4,68},{5,7},{6,70},{7,1},{8,72},{9,11},... | collective-permute-start | bytes 1966088 | tf_op jit(solution)/shard_map/ppermute | solution.py:41
  33.4 6.7 %collective-permute-start.5 = (bf16[256,256]{1,0:T(8,128)(2,1)}, bf16[256,256]{1,0:T(8,128)(2,1)S(1)}, u32[]{:S(2)}, u32[]{:S(2)}) collective-permute-start(bf16[256,256]{1,0:T(8,128)(2,1)} %copy-done.9), channel_id=1, source_target_pairs={{0,16},{1,17},{2,18},{3,19},{4,20},{5,21},{6,22},{7,23},{8,24},{9,... | collective-permute-start | bytes 393224 | tf_op jit(solution)/shard_map/ppermute | solution.py:41
  35.8 7.5 %collective-permute-start.4 = (bf16[256,256]{1,0:T(8,128)(2,1)}, bf16[256,256]{1,0:T(8,128)(2,1)}, u32[]{:S(2)}, u32[]{:S(2)}) collective-permute-start(bf16[256,256]{1,0:T(8,128)(2,1)} %copy-done.9), channel_id=1, source_target_pairs={{0,8},{1,9},{2,10},{3,11},{4,12},{5,13},{6,14},{7,15},{8,16},{9,17... | collective-permute-start | bytes 393224 | tf_op jit(solution)/shard_map/ppermute | solution.py:41
  45.1 15.1 %collective-permute-start.17 = (bf16[768,256]{1,0:T(8,128)(2,1)}, bf16[768,256]{1,0:T(8,128)(2,1)S(1)}, u32[]{:S(2)}, u32[]{:S(2)}) collective-permute-start(bf16[768,256]{1,0:T(8,128)(2,1)} %join.2), channel_id=1, source_target_pairs={{0,192},{1,7},{2,194},{3,1},{4,196},{5,3},{6,198},{7,5},{8,200},{9... | collective-permute-start | bytes 1179656 | tf_op jit(solution)/shard_map/ppermute | solution.py:41
  47.2 13.1 %collective-permute-start.15 = (bf16[768,256]{1,0:T(8,128)(2,1)}, bf16[768,256]{1,0:T(8,128)(2,1)S(1)}, u32[]{:S(2)}, u32[]{:S(2)}) collective-permute-start(bf16[768,256]{1,0:T(8,128)(2,1)} %join.2), channel_id=1, source_target_pairs={{0,64},{1,3},{2,66},{3,5},{4,68},{5,7},{6,70},{7,1},{8,72},{9,11},... | collective-permute-start | bytes 1179656 | tf_op jit(solution)/shard_map/ppermute | solution.py:41
  54.6 18.3 %collective-permute-start.19 = (bf16[1280,256]{1,0:T(8,128)(2,1)}, bf16[1280,256]{1,0:T(8,128)(2,1)S(1)}, u32[]{:S(2)}, u32[]{:S(2)}) collective-permute-start(bf16[1280,256]{1,0:T(8,128)(2,1)} %join.3), channel_id=1, source_target_pairs={{0,192},{1,7},{2,194},{3,1},{4,196},{5,3},{6,198},{7,5},{8,200},{9... | collective-permute-start | bytes 1966088 | tf_op jit(solution)/shard_map/ppermute | solution.py:41
  54.6 22.2 %collective-permute-start.16 = (bf16[1280,256]{1,0:T(8,128)(2,1)}, bf16[1280,256]{1,0:T(8,128)(2,1)S(1)}, u32[]{:S(2)}, u32[]{:S(2)}) collective-permute-start(bf16[1280,256]{1,0:T(8,128)(2,1)} %collective-permute-done.14), channel_id=1, source_target_pairs={{0,64},{1,3},{2,66},{3,5},{4,68},{5,7},{6,70},{7,1},{8,72},{9,11},... | collective-permute-start | bytes 1966088 | tf_op jit(solution)/shard_map/ppermute | solution.py:41
  57.2 19.6 %collective-permute-start.11 = (bf16[16,128,128]{2,1,0:T(8,128)(2,1)S(1)}, bf16[16,128,128]{2,1,0:T(8,128)(2,1)S(1)}, u32[]{:S(2)}, u32[]{:S(2)}) collective-permute-start(bf16[16,128,128]{2,1,0:T(8,128)(2,1)S(1)} %slice.9), channel_id=1, source_target_pairs={{0,6},{1,193},{2,0},{3,195},{4,2},{5,197},{6,4},{7,199},{8,14},{9,... | collective-permute-start | bytes 1572872 | tf_op jit(solution)/shard_map/ppermute | solution.py:41
  60.3 16.6 %collective-permute-start.9 = (bf16[16,128,128]{2,1,0:T(8,128)(2,1)S(1)}, bf16[16,128,128]{2,1,0:T(8,128)(2,1)S(1)}, u32[]{:S(2)}, u32[]{:S(2)}) collective-permute-start(bf16[16,128,128]{2,1,0:T(8,128)(2,1)S(1)} %slice.8), channel_id=1, source_target_pairs={{0,2},{1,65},{2,4},{3,67},{4,6},{5,69},{6,0},{7,71},{8,10},{9,73},... | collective-permute-start | bytes 1572872 | tf_op jit(solution)/shard_map/ppermute | solution.py:41
  60.3 16.6 %collective-permute-start.18 = (bf16[768,256]{1,0:T(8,128)(2,1)S(1)}, bf16[768,256]{1,0:T(8,128)(2,1)S(1)}, u32[]{:S(2)}, u32[]{:S(2)}) collective-permute-start(bf16[768,256]{1,0:T(8,128)(2,1)S(1)} %collective-permute-done.17), channel_id=1, source_target_pairs={{0,192},{1,7},{2,194},{3,1},{4,196},{5,3},{6,198},{7,5},{8,200},{9... | collective-permute-start | bytes 1179656 | tf_op jit(solution)/shard_map/ppermute | solution.py:41
  82.6 4.1 %collective-permute-start.24 = (f32[32,256]{1,0:T(8,128)S(1)}, f32[32,256]{1,0:T(8,128)S(1)}, u32[]{:S(2)}, u32[]{:S(2)}) collective-permute-start(f32[32,256]{1,0:T(8,128)S(1)} %get-tuple-element.47), channel_id=1, source_target_pairs={{0,64},{1,3},{2,66},{3,5},{4,68},{5,7},{6,70},{7,1},{8,72},{9,11},... | collective-permute-start | bytes 98312 | tf_op jit(solution)/shard_map/ppermute | solution.py:41
  84.4 4.3 %collective-permute-start.23 = (f32[32,256]{1,0:T(8,128)S(1)}, f32[32,256]{1,0:T(8,128)S(1)}, u32[]{:S(2)}, u32[]{:S(2)}) collective-permute-start(f32[32,256]{1,0:T(8,128)S(1)} %get-tuple-element.47), channel_id=1, source_target_pairs={{0,128},{1,5},{2,130},{3,7},{4,132},{5,1},{6,134},{7,3},{8,136},{9... | collective-permute-start | bytes 98312 | tf_op jit(solution)/shard_map/ppermute | solution.py:41
  88.6 6.9 %collective-permute-start.26 = (f32[32,256]{1,0:T(8,128)S(1)}, f32[32,256]{1,0:T(8,128)S(1)}, u32[]{:S(2)}, u32[]{:S(2)}) collective-permute-start(f32[32,256]{1,0:T(8,128)S(1)} %add_add_fusion.1), channel_id=1, source_target_pairs={{0,32},{1,33},{2,34},{3,35},{4,36},{5,37},{6,38},{7,39},{8,40},{9,... | collective-permute-start | bytes 98312 | tf_op jit(solution)/shard_map/ppermute | solution.py:41
  95.5 4.1 %collective-permute-start.28 = (f32[32,256]{1,0:T(8,128)S(1)}, f32[32,256]{1,0:T(8,128)S(1)}, u32[]{:S(2)}, u32[]{:S(2)}) collective-permute-start(f32[32,256]{1,0:T(8,128)S(1)} %add.27), channel_id=1, source_target_pairs={{0,8},{1,9},{2,10},{3,11},{4,12},{5,13},{6,14},{7,15},{8,16},{9,17... | collective-permute-start | bytes 98312 | tf_op jit(solution)/shard_map/ppermute | solution.py:41
  97.0 5.0 %collective-permute-start.27 = (f32[32,256]{1,0:T(8,128)S(1)}, f32[32,256]{1,0:T(8,128)S(1)}, u32[]{:S(2)}, u32[]{:S(2)}) collective-permute-start(f32[32,256]{1,0:T(8,128)S(1)} %add.27), channel_id=1, source_target_pairs={{0,16},{1,17},{2,18},{3,19},{4,20},{5,21},{6,22},{7,23},{8,24},{9,... | collective-permute-start | bytes 98312 | tf_op jit(solution)/shard_map/ppermute | solution.py:41
  97.0 12.7 %collective-permute-start.20 = (f32[128,256]{1,0:T(8,128)S(1)}, f32[128,256]{1,0:T(8,128)S(1)}, u32[]{:S(2)}, u32[]{:S(2)}) collective-permute-start(f32[128,256]{1,0:T(8,128)S(1)} %get-tuple-element.44), channel_id=1, source_target_pairs={{0,6},{1,193},{2,0},{3,195},{4,2},{5,197},{6,4},{7,199},{8,14},{9,... | collective-permute-start | bytes 393224 | tf_op jit(solution)/shard_map/ppermute | solution.py:41
  97.0 12.7 %collective-permute-start.21 = (f32[128,256]{1,0:T(8,128)S(1)}, f32[128,256]{1,0:T(8,128)S(1)}, u32[]{:S(2)}, u32[]{:S(2)}) collective-permute-start(f32[128,256]{1,0:T(8,128)S(1)} %get-tuple-element.45), channel_id=1, source_target_pairs={{0,2},{1,65},{2,4},{3,67},{4,6},{5,69},{6,0},{7,71},{8,10},{9,73},... | collective-permute-start | bytes 393224 | tf_op jit(solution)/shard_map/ppermute | solution.py:41
  98.5 11.2 %collective-permute-start.22 = (f32[128,256]{1,0:T(8,128)S(1)}, f32[128,256]{1,0:T(8,128)S(1)}, u32[]{:S(2)}, u32[]{:S(2)}) collective-permute-start(f32[128,256]{1,0:T(8,128)S(1)} %get-tuple-element.46), channel_id=1, source_target_pairs={{0,4},{1,129},{2,6},{3,131},{4,0},{5,133},{6,2},{7,135},{8,12},{9,... | collective-permute-start | bytes 393224 | tf_op jit(solution)/shard_map/ppermute | solution.py:41
  102.0 4.5 %collective-permute-start.32 = (f32[32,256]{1,0:T(8,128)S(1)}, f32[32,256]{1,0:T(8,128)S(1)}, u32[]{:S(2)}, u32[]{:S(2)}) collective-permute-start(f32[32,256]{1,0:T(8,128)S(1)} %add_add_fusion.refs_0_), channel_id=1, source_target_pairs={{0,4},{1,129},{2,6},{3,131},{4,0},{5,133},{6,2},{7,135},{8,12},{9,... | collective-permute-start | bytes 98312 | tf_op jit(solution)/shard_map/ppermute | solution.py:41
  102.1 4.5 %collective-permute-start.31 = (f32[32,256]{1,0:T(8,128)S(1)}, f32[32,256]{1,0:T(8,128)S(1)}, u32[]{:S(2)}, u32[]{:S(2)}) collective-permute-start(f32[32,256]{1,0:T(8,128)S(1)} %add_add_fusion.refs_0_), channel_id=1, source_target_pairs={{0,2},{1,65},{2,4},{3,67},{4,6},{5,69},{6,0},{7,71},{8,10},{9,73},... | collective-permute-start | bytes 98312 | tf_op jit(solution)/shard_map/ppermute | solution.py:41
  109.7 11.1 %collective-permute-start.33 = (f32[128,256]{1,0:T(8,128)S(1)}, f32[128,256]{1,0:T(8,128)S(1)}, u32[]{:S(2)}, u32[]{:S(2)}) collective-permute-start(f32[128,256]{1,0:T(8,128)S(1)} %get-tuple-element.48.refs_0_), channel_id=1, source_target_pairs={{0,1},{1,0},{2,3},{3,2},{4,5},{5,4},{6,7},{7,6},{8,9},{9,8},{10,11... | collective-permute-start | bytes 393224 | tf_op jit(solution)/shard_map/ppermute | solution.py:41
  116.7 4.1 %collective-permute-start.34 = (f32[128,256]{1,0:T(8,128)S(1)}, f32[128,256]{1,0:T(8,128)S(1)}, u32[]{:S(2)}, u32[]{:S(2)}) collective-permute-start(f32[128,256]{1,0:T(8,128)S(1)} %collective-permute-done.20.refs_1_), channel_id=1, source_target_pairs={{0,1},{1,0},{2,3},{3,2},{4,5},{5,4},{6,7},{7,6},{8,9},{9,8},{10,11... | collective-permute-start | bytes 393224 | tf_op jit(solution)/shard_map/ppermute | solution.py:41
  116.8 4.0 %collective-permute-start.35 = (f32[128,256]{1,0:T(8,128)S(1)}, f32[128,256]{1,0:T(8,128)S(1)}, u32[]{:S(2)}, u32[]{:S(2)}) collective-permute-start(f32[128,256]{1,0:T(8,128)S(1)} %collective-permute-done.21.refs_2_), channel_id=1, source_target_pairs={{0,1},{1,0},{2,3},{3,2},{4,5},{5,4},{6,7},{7,6},{8,9},{9,8},{10,11... | collective-permute-start | bytes 393224 | tf_op jit(solution)/shard_map/ppermute | solution.py:41
  (22 other events, 280.3 us)
where the time goes:
time: 123 us
  starting transfers between devices  51.7 us (42%)
  waiting for transfers between devices  45.1 us (37%)
  Pallas kernels  16.8 us (14%)
  local copies, waits for them, and re-layouts  5.11 us (4%)
  between operations  1.71 us (1%)
  matrix products  1.65 us (1%)
    ppermute x38, starting transfers between devices, send(): return lax.ppermute(value, AXES, pairs_of(role, step))  51.7 us
    ppermute x38, waiting for transfers between devices, send(): return lax.ppermute(value, AXES, pairs_of(role, step))  45.1 us
    pallas_call x1, Pallas kernels, aggregate(): pl.pallas_call(aggregate_kernel, in_specs=[SMEM, VMEM] + [ANY] * 13, out_...  5.58 us
    pallas_call x2, Pallas kernels, join(): pl.pallas_call(join_kernel, in_specs=[VMEM] * len(pieces), out_specs=VMEM...  3.86 us
    unnamed x32, local copies, waits for them, and re-layouts  2.96 us
  transfers between devices with their start and end apart: 38, of which 16 were waited for; matrix products, arithmetic and copies ran while one was open for 4% of the time, Pallas kernels for 6%

commit v1 on v0

--- a/solution.py
+++ b/solution.py
@@ -128,58 +128,6 @@
         out_shape=[shape] * GROUP,
         name="split",
     )(count, index, ids, grad)
-
-
-def unpack_kernel(*refs):
-    packed, (own, where, ids) = refs[0:GROUP], refs[GROUP:]
-    rep, u, v, z = place()
-    rows = []
-    for s in range(GROUP):
-        own[64 * s : 64 * s + 64, :] = packed[s][0:64, :]
-        rows.append(packed[s][64:80, :].astype(jnp.float32)[0:1])
-    rows = jnp.concatenate(rows, axis=0).astype(jnp.int32)
-    ids[...] = rows[:, 128:256]
-    source = rows[:, 0:128]
-    sx, sz, sy = source & (NX - 1), (source >> 2) & (NZ - 1), source >> 5
-    du = (u - jnp.where(rep == 0, sx, sy)) & (GROUP - 1)
-    dv = (v - jnp.where(rep == 0, sy, sx)) & (GROUP - 1)
-    dz = (z - sz) & (NZ - 1)
-    spot = jnp.zeros_like(dz)
-    for i, p in enumerate((0, 1, 3, 5, 6, 7, 4, 2)):
-        spot = jnp.where(dz == i, p, spot)
-    lane = lax.broadcasted_iota(jnp.int32, (GROUP, 128), 1)
-    count = jnp.max(jnp.where(lane == 64, source, 0), axis=1, keepdims=True)
-    where[...] = jnp.where(lane < count, dv * 32 + spot * 4 + du, EMPTY)
-
-
-def unpack(packed):
-    return pl.pallas_call(
-        unpack_kernel,
-        in_specs=[VMEM] * GROUP,
-        out_specs=[VMEM] * 3,
-        out_shape=[
-            jax.ShapeDtypeStruct((256, 256), jnp.bfloat16),
-            jax.ShapeDtypeStruct((GROUP, 128), jnp.int32),
-            jax.ShapeDtypeStruct((GROUP, 128), jnp.int32),
-        ],
-        name="unpack",
-    )(*packed)
-
-
-def join_kernel(*refs):
-    pieces, out = refs[:-1], refs[-1]
-    for i, piece in enumerate(pieces):
-        out[256 * i : 256 * i + 256, :] = piece[...]
-
-
-def join(*pieces):
-    return pl.pallas_call(
-        join_kernel,
-        in_specs=[VMEM] * len(pieces),
-        out_specs=VMEM,
-        out_shape=jax.ShapeDtypeStruct((256 * len(pieces), 256), jnp.bfloat16),
-        name="join",
-    )(*pieces)
 
 
 def aggregate_kernel(where, ids, *refs):
@@ -331,32 +279,44 @@
     )(weight_self, weight_neigh, *mine)
 
 
-def total_of_four(value, role):
-    near = send(value, role, 1), send(value, role, -1)
-    return (value + send(value, role, 2)) + (near[0] + near[1])
+def total_of_four(value, role, step=1):
+    near = send(value, role, step), send(value, role, -step)
+    return (value + send(value, role, 2 * step)) + (near[0] + near[1])
 
 
 def shards(grad_out, w_self, w_neigh, adj_tiles, tile_index, tile_count, prompt_ids):
     shares = split(tile_count, tile_index, prompt_ids[None, :], grad_out)
     packed = [shares[0]] + [send(shares[s], "u", s) for s in range(1, GROUP)]
+    own = jnp.concatenate([p[0:64] for p in packed], axis=0)
+
     mine = pack(adj_tiles[0])
-    mine, packed = lax.optimization_barrier((mine, packed))
-    own, where, ids = unpack(packed)
     left, right = send(mine, "u", 1), send(mine, "u", -1)
 
     z1, z7, z2, z6 = [send(own, "z", s) for s in (1, -1, 2, -2)]
     z3, z4, z5 = send(z2, "z", 1), send(z2, "z", 2), send(z6, "z", -1)
 
-    near = join(own, z1, z7, z2, z6)
+    near = jnp.concatenate([own, z1, z7, z2, z6], axis=0)
     near_m, near_p = send(near, "v", 1), send(near, "v", -1)
     far = [send(left[0:16], "u", 1), send(right[16:32], "u", -1)]
     tiles = [mine, left, *far, right]
-    rest = join(z3, z4, z5)
+    rest = jnp.concatenate([z3, z4, z5], axis=0)
     self_term, rest = lax.optimization_barrier((dot_t(grad_out, w_self), rest))
     rest_m, rest_p = send(rest, "v", 1), send(rest, "v", -1)
     near_2, rest_2 = send(near_m, "v", 1), send(rest_p, "v", -1)
     chunks = [near, rest, near_m, rest_m, near_2, rest_2, near_p, rest_p]
     chunks = [c.reshape(c.shape[0] // 64, 64, 256) for c in chunks]
+
+    rep, u, v, z = place()
+    index = jnp.stack([p[64, 0:64] for p in packed]).astype(jnp.int32)
+    count = jnp.stack([p[64, 64:128] for p in packed]).astype(jnp.int32)
+    ids = jnp.stack([p[64, 128:256] for p in packed]).astype(jnp.int32)
+    sx, sz, sy = index % NX, (index // NX) % NZ, index // (NX * NZ)
+    du = (u - jnp.where(rep == 0, sx, sy)) % GROUP
+    dv = (v - jnp.where(rep == 0, sy, sx)) % GROUP
+    dz = (z - sz) % NZ
+    spot = sum(jnp.where(dz == i, p, 0) for i, p in enumerate((0, 1, 3, 5, 6, 7, 4, 2)))
+    where = jnp.where(jnp.arange(64)[None, :] < count, dv * 32 + spot * 4 + du, EMPTY)
+    where = where.astype(jnp.int32)
 
     *parts, sums = aggregate(where, ids, tiles, chunks)
 
@@ -368,8 +328,8 @@
     ]
 
     sums = total_of_four(sums, "v")
-    sums = sums + send(sums, "z", 4)
-    sums = total_of_four(sums, "z")
+    sums = total_of_four(sums, "z", 2)
+    sums = sums + send(sums, "z", 1)
     pieces = [sums, send(sums, "u", -1), send(sums, "u", 1), send(sums, "u", 2)]
     owned, pieces = lax.optimization_barrier((owned, pieces))
     product = prompt(w_self, w_neigh, pieces)

time: 123 us -> 121 us (0.984)
  waiting for transfers between devices: 45.1 us -> 33.6 us
  local copies, waits for them, and re-layouts: 5.11 us -> 15.6 us
  Pallas kernels: 16.8 us -> 11.1 us
  starting transfers between devices: 51.7 us -> 54.8 us
    ppermute x38, waiting for transfers between devices: 45.1 us -> 33.6 us  [send(): return lax.ppermute(value, AXES, pairs_of(role, step))]
    slice x0 -> x8, local copies, waits for them, and re-layouts: none -> 6.01 us  [the longest x4 3.31 us: shards(): index = jnp.stack([p[64, 0:64] for p in packed]).astype(jnp.int32)]
    pallas_call x3 -> x0, Pallas kernels: 5.45 us -> none  [the longest x2 3.86 us: join(): pl.pallas_call(join_kernel, in_specs=[VMEM] * len(pieces), out_specs=VMEM...]
    unnamed x32 -> x23, local copies, waits for them, and re-layouts: 2.96 us -> 6.8 us
    ppermute x38, starting transfers between devices: 51.7 us -> 54.8 us  [send(): return lax.ppermute(value, AXES, pairs_of(role, step))]
  transfers between devices with their start and end apart: 38 -> 38, of which waited for: 16 -> 14; matrix products, arithmetic and copies ran while one was open for 4% -> 14% of each run, Pallas kernels for 6% -> 2%
where the time goes in v1:
time: 121 us; the launch traced here: 120 us
  starting transfers between devices  54.8 us (45%)
  waiting for transfers between devices  33.6 us (28%)
  local copies, waits for them, and re-layouts  15.6 us (13%)
  Pallas kernels  11.1 us (9%)
  other arithmetic  1.66 us (1%)
  matrix products  1.63 us (1%)
  between operations  1.62 us (1%)
    ppermute x38, starting transfers between devices, send(): return lax.ppermute(value, AXES, pairs_of(role, step))  54.8 us
    ppermute x38, waiting for transfers between devices, send(): return lax.ppermute(value, AXES, pairs_of(role, step))  33.6 us
    unnamed x23, local copies, waits for them, and re-layouts  6.8 us
    pallas_call x1, Pallas kernels, aggregate(): pl.pallas_call(aggregate_kernel, in_specs=[SMEM, VMEM] + [ANY] * 13, out_...  5.39 us
    slice x4, local copies, waits for them, and re-layouts, shards(): index = jnp.stack([p[64, 0:64] for p in packed]).astype(jnp.int32)  3.31 us
    slice x4, local copies, waits for them, and re-layouts, shards(): ids = jnp.stack([p[64, 128:256] for p in packed]).astype(jnp.int32)  2.7 us
  transfers between devices with their start and end apart: 38, of which 14 were waited for; matrix products, arithmetic and copies ran while one was open for 14% of the time, Pallas kernels for 2%

profile of v1, /device:TPU:1, one launch (start us, length us, event | category | flops | bytes accessed | tf_op | source)
XLA Modules:
  0.0 120.0 jit_solution(7957075566747667009)
XLA Ops:
  1.3 1.7 %split.1 = (bf16[80,256]{1,0:T(8,128)(2,1)}, bf16[80,256]{1,0:T(8,128)(2,1)}, bf16[80,256]{1,0:T(8,128)(2,1)}, bf16[80,256]{1,0:T(8,128)(2,1)}) custom-call(s32[1]{0:T(128)S(6)} %copy.16.count, s32[1,64]{1,0:T(1,128)} %index.1, s32[1,128]{1,0:T(1,128)} %bitcast.19, bf16[128,1024]{1,0:T(8,128)(2,1)} %grad.1), custom_call_target="tpu_custom_call" | custom-call | tf_op jit(solution)/shard_map/split/pallas_call | solution.py:124
  2.9 2.1 %collective-permute-start = (bf16[80,256]{1,0:T(8,128)(2,1)}, bf16[80,256]{1,0:T(8,128)(2,1)S(1)}, u32[]{:S(2)}, u32[]{:S(2)}) collective-permute-start(bf16[80,256]{1,0:T(8,128)(2,1)} %get-tuple-element.22), channel_id=1, source_target_pairs={{0,2},{1,65},{2,4},{3,67},{4,6},{5,69},{6,0},{7,71},{8,10},{9,73},... | collective-permute-start | bytes 122888 | tf_op jit(solution)/shard_map/ppermute | solution.py:41
  5.1 2.6 %collective-permute-start.1 = (bf16[80,256]{1,0:T(8,128)(2,1)}, bf16[80,256]{1,0:T(8,128)(2,1)S(1)}, u32[]{:S(2)}, u32[]{:S(2)}) collective-permute-start(bf16[80,256]{1,0:T(8,128)(2,1)} %get-tuple-element.23), channel_id=1, source_target_pairs={{0,4},{1,129},{2,6},{3,131},{4,0},{5,133},{6,2},{7,135},{8,12},{9,... | collective-permute-start | bytes 122888 | tf_op jit(solution)/shard_map/ppermute | solution.py:41
  8.8 1.4 %constant_dynamic-update-slice_fusion.7 = (bf16[1280,256]{1,0:T(8,128)(2,1)}, bf16[64,256]{1,0:T(8,128)(2,1)S(1)}) fusion(bf16[80,256]{1,0:T(8,128)(2,1)} %get-tuple-element.21), kind=kLoop, calls=%fused_computation.11 | loop fusion | bytes 98304
  12.0 1.7 %collective-permute-start.12 = (bf16[256,256]{1,0:T(8,128)(2,1)S(1)}, bf16[256,256]{1,0:T(8,128)(2,1)S(1)}, u32[]{:S(2)}, u32[]{:S(2)}) collective-permute-start(bf16[256,256]{1,0:T(8,128)(2,1)S(1)} %pad_maximum_fusion.1), channel_id=1, source_target_pairs={{0,8},{1,9},{2,10},{3,11},{4,12},{5,13},{6,14},{7,15},{8,16},{9,17... | collective-permute-start | bytes 393224 | tf_op jit(solution)/shard_map/ppermute | solution.py:41
  13.7 5.1 %collective-permute-start.6 = (bf16[256,256]{1,0:T(8,128)(2,1)S(1)}, bf16[256,256]{1,0:T(8,128)(2,1)S(1)}, u32[]{:S(2)}, u32[]{:S(2)}) collective-permute-start(bf16[256,256]{1,0:T(8,128)(2,1)S(1)} %pad_maximum_fusion.1), channel_id=1, source_target_pairs={{0,48},{1,49},{2,50},{3,51},{4,52},{5,53},{6,54},{7,55},{8,56},{9,... | collective-permute-start | bytes 393224 | tf_op jit(solution)/shard_map/ppermute | solution.py:41
  19.6 1.6 %copy-done.2 = bf16[1,64,128,128]{3,2,1,0:T(8,128)(2,1)S(1)} copy-done((bf16[1,64,128,128]{3,2,1,0:T(8,128)(2,1)S(1)}, bf16[1,64,128,128]{3,2,1,0:T(8,128)(2,1)}, u32[]{:S(2)}) %copy-start.2) | copy-done | bytes 2097176
  22.1 1.7 %collective-permute-start.10 = (bf16[32,128,128]{2,1,0:T(8,128)(2,1)S(1)}, bf16[32,128,128]{2,1,0:T(8,128)(2,1)}, u32[]{:S(2)}, u32[]{:S(2)}) collective-permute-start(bf16[32,128,128]{2,1,0:T(8,128)(2,1)S(1)} %pack.1.refs_0_), channel_id=1, source_target_pairs={{0,6},{1,193},{2,0},{3,195},{4,2},{5,197},{6,4},{7,199},{8,14},{9,... | collective-permute-start | bytes 3145736 | tf_op jit(solution)/shard_map/ppermute | solution.py:41
  24.4 2.6 %collective-permute-start.7 = (bf16[256,256]{1,0:T(8,128)(2,1)S(1)}, bf16[256,256]{1,0:T(8,128)(2,1)S(1)}, u32[]{:S(2)}, u32[]{:S(2)}) collective-permute-start(bf16[256,256]{1,0:T(8,128)(2,1)S(1)} %collective-permute-done.6), channel_id=1, source_target_pairs={{0,56},{1,57},{2,58},{3,59},{4,60},{5,61},{6,62},{7,63},{8,0},{9,1... | collective-permute-start | bytes 393224 | tf_op jit(solution)/shard_map/ppermute | solution.py:41
  28.2 2.2 %collective-permute-done.3 = bf16[256,256]{1,0:T(8,128)(2,1)S(1)} collective-permute-done((bf16[256,256]{1,0:T(8,128)(2,1)S(1)}, bf16[256,256]{1,0:T(8,128)(2,1)S(1)}, u32[]{:S(2)}, u32[]{:S(2)}) %collective-permute-start.3) | collective-permute-done | bytes 131104 | tf_op jit(solution)/shard_map/ppermute | solution.py:41
  31.8 1.6 %collective-permute-start.14 = (bf16[1280,256]{1,0:T(8,128)(2,1)}, bf16[1280,256]{1,0:T(8,128)(2,1)}, u32[]{:S(2)}, u32[]{:S(2)}) collective-permute-start(bf16[1280,256]{1,0:T(8,128)(2,1)} %constant_dynamic-update-slice_fusion), channel_id=1, source_target_pairs={{0,64},{1,3},{2,66},{3,5},{4,68},{5,7},{6,70},{7,1},{8,72},{9,11},... | collective-permute-start | bytes 1966088 | tf_op jit(solution)/shard_map/ppermute | solution.py:41
  33.4 1.3 %collective-permute-start.4 = (bf16[256,256]{1,0:T(8,128)(2,1)S(1)}, bf16[256,256]{1,0:T(8,128)(2,1)}, u32[]{:S(2)}, u32[]{:S(2)}) collective-permute-start(bf16[256,256]{1,0:T(8,128)(2,1)S(1)} %collective-permute-done.3), channel_id=1, source_target_pairs={{0,8},{1,9},{2,10},{3,11},{4,12},{5,13},{6,14},{7,15},{8,16},{9,17... | collective-permute-start | bytes 393224 | tf_op jit(solution)/shard_map/ppermute | solution.py:41
  34.7 1.6 %fusion.16.self_term = f32[128,1024]{1,0:T(8,128)} fusion(bf16[128,1024]{1,0:T(8,128)(2,1)S(1)} %copy-done.4, bf16[1024,1024]{1,0:T(8,128)(2,1)S(1)} %copy-done), kind=kOutput, calls=%fused_computation.53 | convolution fusion | flops 268435456 | bytes 2883584 | tf_op jit(solution)/shard_map/dot_general | solution.py:225
  37.0 3.7 %collective-permute-done.5 = bf16[256,256]{1,0:T(8,128)(2,1)S(1)} collective-permute-done((bf16[256,256]{1,0:T(8,128)(2,1)S(1)}, bf16[256,256]{1,0:T(8,128)(2,1)S(1)}, u32[]{:S(2)}, u32[]{:S(2)}) %collective-permute-start.5) | collective-permute-done | bytes 131104 | tf_op jit(solution)/shard_map/ppermute | solution.py:41
  40.8 1.8 %collective-permute-done.4 = bf16[256,256]{1,0:T(8,128)(2,1)} collective-permute-done((bf16[256,256]{1,0:T(8,128)(2,1)S(1)}, bf16[256,256]{1,0:T(8,128)(2,1)}, u32[]{:S(2)}, u32[]{:S(2)}) %collective-permute-start.4) | collective-permute-done | bytes 131104 | tf_op jit(solution)/shard_map/ppermute | solution.py:41
  43.5 1.3 %collective-permute-start.17 = (bf16[768,256]{1,0:T(8,128)(2,1)S(1)}, bf16[768,256]{1,0:T(8,128)(2,1)S(1)}, u32[]{:S(2)}, u32[]{:S(2)}) collective-permute-start(bf16[768,256]{1,0:T(8,128)(2,1)S(1)} %pad_maximum_fusion), channel_id=1, source_target_pairs={{0,192},{1,7},{2,194},{3,1},{4,196},{5,3},{6,198},{7,5},{8,200},{9... | collective-permute-start | bytes 1179656 | tf_op jit(solution)/shard_map/ppermute | solution.py:41
  47.2 2.4 %collective-permute-done.14 = bf16[1280,256]{1,0:T(8,128)(2,1)} collective-permute-done((bf16[1280,256]{1,0:T(8,128)(2,1)}, bf16[1280,256]{1,0:T(8,128)(2,1)}, u32[]{:S(2)}, u32[]{:S(2)}) %collective-permute-start.14) | collective-permute-done | bytes 655392 | tf_op jit(solution)/shard_map/ppermute | solution.py:41
  49.6 1.5 %collective-permute-start.16 = (bf16[1280,256]{1,0:T(8,128)(2,1)}, bf16[1280,256]{1,0:T(8,128)(2,1)S(1)}, u32[]{:S(2)}, u32[]{:S(2)}) collective-permute-start(bf16[1280,256]{1,0:T(8,128)(2,1)} %collective-permute-done.14), channel_id=1, source_target_pairs={{0,64},{1,3},{2,66},{3,5},{4,68},{5,7},{6,70},{7,1},{8,72},{9,11},... | collective-permute-start | bytes 1966088 | tf_op jit(solution)/shard_map/ppermute | solution.py:41
  52.2 2.9 %collective-permute-start.11 = (bf16[16,128,128]{2,1,0:T(8,128)(2,1)S(1)}, bf16[16,128,128]{2,1,0:T(8,128)(2,1)S(1)}, u32[]{:S(2)}, u32[]{:S(2)}) collective-permute-start(bf16[16,128,128]{2,1,0:T(8,128)(2,1)S(1)} %slice.85), channel_id=1, source_target_pairs={{0,6},{1,193},{2,0},{3,195},{4,2},{5,197},{6,4},{7,199},{8,14},{9,... | collective-permute-start | bytes 1572872 | tf_op jit(solution)/shard_map/ppermute | solution.py:41
  61.2 9.0 %collective-permute-done.18 = bf16[768,256]{1,0:T(8,128)(2,1)S(1)} collective-permute-done((bf16[768,256]{1,0:T(8,128)(2,1)S(1)}, bf16[768,256]{1,0:T(8,128)(2,1)S(1)}, u32[]{:S(2)}, u32[]{:S(2)}) %collective-permute-start.18) | collective-permute-done | bytes 393248 | tf_op jit(solution)/shard_map/ppermute | solution.py:41
  71.4 5.4 %aggregate.1 = (f32[128,256]{1,0:T(8,128)S(1)}, f32[128,256]{1,0:T(8,128)S(1)}, f32[128,256]{1,0:T(8,128)S(1)}, f32[128,256]{1,0:T(8,128)S(1)}, f32[32,256]{1,0:T(8,128)S(1)}) custom-call(s32[4,64]{1,0:T(4,128)S(1)} %fusion.5.where, s32[4,128]{1,0:T(4,128)S(1)} %maximum_convert_fusion.ids, bf16[32,128,128]{2,1,0:T(8,128)(2,1)S(1)} %pack.1.refs_0_, ...), custom_call_target="tpu_custom_call" | custom-call | tf_op jit(solution)/shard_map/aggregate/pallas_call | solution.py:187
  79.7 2.4 %collective-permute-done.24 = f32[32,256]{1,0:T(8,128)S(1)} collective-permute-done((f32[32,256]{1,0:T(8,128)S(1)}, f32[32,256]{1,0:T(8,128)S(1)}, u32[]{:S(2)}, u32[]{:S(2)}) %collective-permute-start.24) | collective-permute-done | bytes 32800 | tf_op jit(solution)/shard_map/ppermute | solution.py:41
  85.1 1.8 %collective-permute-start.26 = (f32[32,256]{1,0:T(8,128)S(1)}, f32[32,256]{1,0:T(8,128)S(1)}, u32[]{:S(2)}, u32[]{:S(2)}) collective-permute-start(f32[32,256]{1,0:T(8,128)S(1)} %add_add_fusion.1), channel_id=1, source_target_pairs={{0,32},{1,33},{2,34},{3,35},{4,36},{5,37},{6,38},{7,39},{8,40},{9,... | collective-permute-start | bytes 98312 | tf_op jit(solution)/shard_map/ppermute | solution.py:41
  87.0 2.0 %collective-permute-start.20 = (f32[128,256]{1,0:T(8,128)S(1)}, f32[128,256]{1,0:T(8,128)S(1)}, u32[]{:S(2)}, u32[]{:S(2)}) collective-permute-start(f32[128,256]{1,0:T(8,128)S(1)} %get-tuple-element.28), channel_id=1, source_target_pairs={{0,6},{1,193},{2,0},{3,195},{4,2},{5,197},{6,4},{7,199},{8,14},{9,... | collective-permute-start | bytes 393224 | tf_op jit(solution)/shard_map/ppermute | solution.py:41
  90.2 1.6 %collective-permute-done.26 = f32[32,256]{1,0:T(8,128)S(1)} collective-permute-done((f32[32,256]{1,0:T(8,128)S(1)}, f32[32,256]{1,0:T(8,128)S(1)}, u32[]{:S(2)}, u32[]{:S(2)}) %collective-permute-start.26) | collective-permute-done | bytes 32800 | tf_op jit(solution)/shard_map/ppermute | solution.py:41
  92.6 3.8 %collective-permute-done.29 = f32[32,256]{1,0:T(8,128)S(1)} collective-permute-done((f32[32,256]{1,0:T(8,128)S(1)}, f32[32,256]{1,0:T(8,128)S(1)}, u32[]{:S(2)}, u32[]{:S(2)}) %collective-permute-start.29) | collective-permute-done | bytes 32800 | tf_op jit(solution)/shard_map/ppermute | solution.py:41
  98.7 2.3 %collective-permute-done.32.refs_3_ = f32[32,256]{1,0:T(8,128)S(1)} collective-permute-done((f32[32,256]{1,0:T(8,128)S(1)}, f32[32,256]{1,0:T(8,128)S(1)}, u32[]{:S(2)}, u32[]{:S(2)}) %collective-permute-start.32) | collective-permute-done | bytes 32800 | tf_op jit(solution)/shard_map/ppermute | solution.py:41
  101.0 1.4 %collective-permute-start.30 = (f32[32,256]{1,0:T(8,128)S(1)}, f32[32,256]{1,0:T(8,128)S(1)}, u32[]{:S(2)}, u32[]{:S(2)}) collective-permute-start(f32[32,256]{1,0:T(8,128)S(1)} %add.92.refs_0_), channel_id=1, source_target_pairs={{0,6},{1,193},{2,0},{3,195},{4,2},{5,197},{6,4},{7,199},{8,14},{9,... | collective-permute-start | bytes 98312 | tf_op jit(solution)/shard_map/ppermute | solution.py:41
  102.4 1.3 %collective-permute-done.30.refs_1_ = f32[32,256]{1,0:T(8,128)S(1)} collective-permute-done((f32[32,256]{1,0:T(8,128)S(1)}, f32[32,256]{1,0:T(8,128)S(1)}, u32[]{:S(2)}, u32[]{:S(2)}) %collective-permute-start.30) | collective-permute-done | bytes 32800 | tf_op jit(solution)/shard_map/ppermute | solution.py:41
  103.8 10.2 %collective-permute-start.33 = (f32[128,256]{1,0:T(8,128)S(1)}, f32[128,256]{1,0:T(8,128)S(1)}, u32[]{:S(2)}, u32[]{:S(2)}) collective-permute-start(f32[128,256]{1,0:T(8,128)S(1)} %get-tuple-element.32.refs_0_), channel_id=1, source_target_pairs={{0,1},{1,0},{2,3},{3,2},{4,5},{5,4},{6,7},{7,6},{8,9},{9,8},{10,11... | collective-permute-start | bytes 393224 | tf_op jit(solution)/shard_map/ppermute | solution.py:41
  114.6 1.4 %prompt.1 = f32[16,1024]{1,0:T(8,128)S(1)} custom-call(bf16[1024,1024]{1,0:T(8,128)(2,1)S(1)} %copy-done, bf16[1024,1024]{1,0:T(8,128)(2,1)S(1)} %copy-done.1, f32[32,256]{1,0:T(8,128)S(1)} %add.92.refs_0_, f32[32,256]{1,0:T(8,128)S(1)} %collective-permute-done.30.refs_1_, f32[32,256]{1,0:T(8,128)S(1)} %collective-permute-done.31.refs_2_, ...), custom_call_target="tpu_custom_call" | custom-call | tf_op jit(solution)/shard_map/prompt/pallas_call | solution.py:268
  118.1 1.8 %finish.1 = bf16[128,1024]{1,0:T(8,128)(2,1)} custom-call(f32[128,1024]{1,0:T(8,128)S(1)} %copy-done.3, bf16[1024,1024]{1,0:T(8,128)(2,1)S(1)} %copy-done.1, f32[128,256]{1,0:T(8,128)S(1)} %get-tuple-element.32.refs_0_, f32[128,256]{1,0:T(8,128)S(1)} %collective-permute-done.20.refs_1_, f32[128,256]{1,0:T(8,128)S(1)} %collective-permute-done.21.refs_2_, ...), custom_call_target="tpu_custom_call" | custom-call | tf_op jit(solution)/shard_map/finish/pallas_call | solution.py:236
  (92 shorter events, 33.1 us)
Async XLA Ops:
  2.9 7.2 %collective-permute-start = (bf16[80,256]{1,0:T(8,128)(2,1)}, bf16[80,256]{1,0:T(8,128)(2,1)S(1)}, u32[]{:S(2)}, u32[]{:S(2)}) collective-permute-start(bf16[80,256]{1,0:T(8,128)(2,1)} %get-tuple-element.22), channel_id=1, source_target_pairs={{0,2},{1,65},{2,4},{3,67},{4,6},{5,69},{6,0},{7,71},{8,10},{9,73},... | collective-permute-start | bytes 122888 | tf_op jit(solution)/shard_map/ppermute | solution.py:41
  5.1 5.7 %collective-permute-start.1 = (bf16[80,256]{1,0:T(8,128)(2,1)}, bf16[80,256]{1,0:T(8,128)(2,1)S(1)}, u32[]{:S(2)}, u32[]{:S(2)}) collective-permute-start(bf16[80,256]{1,0:T(8,128)(2,1)} %get-tuple-element.23), channel_id=1, source_target_pairs={{0,4},{1,129},{2,6},{3,131},{4,0},{5,133},{6,2},{7,135},{8,12},{9,... | collective-permute-start | bytes 122888 | tf_op jit(solution)/shard_map/ppermute | solution.py:41
  12.0 11.8 %collective-permute-start.12 = (bf16[256,256]{1,0:T(8,128)(2,1)S(1)}, bf16[256,256]{1,0:T(8,128)(2,1)S(1)}, u32[]{:S(2)}, u32[]{:S(2)}) collective-permute-start(bf16[256,256]{1,0:T(8,128)(2,1)S(1)} %pad_maximum_fusion.1), channel_id=1, source_target_pairs={{0,8},{1,9},{2,10},{3,11},{4,12},{5,13},{6,14},{7,15},{8,16},{9,17... | collective-permute-start | bytes 393224 | tf_op jit(solution)/shard_map/ppermute | solution.py:41
  13.7 10.6 %collective-permute-start.6 = (bf16[256,256]{1,0:T(8,128)(2,1)S(1)}, bf16[256,256]{1,0:T(8,128)(2,1)S(1)}, u32[]{:S(2)}, u32[]{:S(2)}) collective-permute-start(bf16[256,256]{1,0:T(8,128)(2,1)S(1)} %pad_maximum_fusion.1), channel_id=1, source_target_pairs={{0,48},{1,49},{2,50},{3,51},{4,52},{5,53},{6,54},{7,55},{8,56},{9,... | collective-permute-start | bytes 393224 | tf_op jit(solution)/shard_map/ppermute | solution.py:41
  18.8 8.8 %collective-permute-start.13 = (bf16[256,256]{1,0:T(8,128)(2,1)S(1)}, bf16[256,256]{1,0:T(8,128)(2,1)S(1)}, u32[]{:S(2)}, u32[]{:S(2)}) collective-permute-start(bf16[256,256]{1,0:T(8,128)(2,1)S(1)} %pad_maximum_fusion.1), channel_id=1, source_target_pairs={{0,56},{1,57},{2,58},{3,59},{4,60},{5,61},{6,62},{7,63},{8,0},{9,1... | collective-permute-start | bytes 393224 | tf_op jit(solution)/shard_map/ppermute | solution.py:41
  22.1 27.6 %collective-permute-start.10 = (bf16[32,128,128]{2,1,0:T(8,128)(2,1)S(1)}, bf16[32,128,128]{2,1,0:T(8,128)(2,1)}, u32[]{:S(2)}, u32[]{:S(2)}) collective-permute-start(bf16[32,128,128]{2,1,0:T(8,128)(2,1)S(1)} %pack.1.refs_0_), channel_id=1, source_target_pairs={{0,6},{1,193},{2,0},{3,195},{4,2},{5,197},{6,4},{7,199},{8,14},{9,... | collective-permute-start | bytes 3145736 | tf_op jit(solution)/shard_map/ppermute | solution.py:41
  23.8 28.4 %collective-permute-start.8 = (bf16[32,128,128]{2,1,0:T(8,128)(2,1)S(1)}, bf16[32,128,128]{2,1,0:T(8,128)(2,1)}, u32[]{:S(2)}, u32[]{:S(2)}) collective-permute-start(bf16[32,128,128]{2,1,0:T(8,128)(2,1)S(1)} %pack.1.refs_0_), channel_id=1, source_target_pairs={{0,2},{1,65},{2,4},{3,67},{4,6},{5,69},{6,0},{7,71},{8,10},{9,73},... | collective-permute-start | bytes 3145736 | tf_op jit(solution)/shard_map/ppermute | solution.py:41
  23.8 6.7 %collective-permute-start.3 = (bf16[256,256]{1,0:T(8,128)(2,1)S(1)}, bf16[256,256]{1,0:T(8,128)(2,1)S(1)}, u32[]{:S(2)}, u32[]{:S(2)}) collective-permute-start(bf16[256,256]{1,0:T(8,128)(2,1)S(1)} %pad_maximum_fusion.1), channel_id=1, source_target_pairs={{0,16},{1,17},{2,18},{3,19},{4,20},{5,21},{6,22},{7,23},{8,24},{9,... | collective-permute-start | bytes 393224 | tf_op jit(solution)/shard_map/ppermute | solution.py:41
  24.4 9.0 %collective-permute-start.7 = (bf16[256,256]{1,0:T(8,128)(2,1)S(1)}, bf16[256,256]{1,0:T(8,128)(2,1)S(1)}, u32[]{:S(2)}, u32[]{:S(2)}) collective-permute-start(bf16[256,256]{1,0:T(8,128)(2,1)S(1)} %collective-permute-done.6), channel_id=1, source_target_pairs={{0,56},{1,57},{2,58},{3,59},{4,60},{5,61},{6,62},{7,63},{8,0},{9,1... | collective-permute-start | bytes 393224 | tf_op jit(solution)/shard_map/ppermute | solution.py:41
  31.8 17.8 %collective-permute-start.14 = (bf16[1280,256]{1,0:T(8,128)(2,1)}, bf16[1280,256]{1,0:T(8,128)(2,1)}, u32[]{:S(2)}, u32[]{:S(2)}) collective-permute-start(bf16[1280,256]{1,0:T(8,128)(2,1)} %constant_dynamic-update-slice_fusion), channel_id=1, source_target_pairs={{0,64},{1,3},{2,66},{3,5},{4,68},{5,7},{6,70},{7,1},{8,72},{9,11},... | collective-permute-start | bytes 1966088 | tf_op jit(solution)/shard_map/ppermute | solution.py:41
  33.4 7.4 %collective-permute-start.5 = (bf16[256,256]{1,0:T(8,128)(2,1)S(1)}, bf16[256,256]{1,0:T(8,128)(2,1)S(1)}, u32[]{:S(2)}, u32[]{:S(2)}) collective-permute-start(bf16[256,256]{1,0:T(8,128)(2,1)S(1)} %collective-permute-done.3), channel_id=1, source_target_pairs={{0,16},{1,17},{2,18},{3,19},{4,20},{5,21},{6,22},{7,23},{8,24},{9,... | collective-permute-start | bytes 393224 | tf_op jit(solution)/shard_map/ppermute | solution.py:41
  33.4 9.1 %collective-permute-start.4 = (bf16[256,256]{1,0:T(8,128)(2,1)S(1)}, bf16[256,256]{1,0:T(8,128)(2,1)}, u32[]{:S(2)}, u32[]{:S(2)}) collective-permute-start(bf16[256,256]{1,0:T(8,128)(2,1)S(1)} %collective-permute-done.3), channel_id=1, source_target_pairs={{0,8},{1,9},{2,10},{3,11},{4,12},{5,13},{6,14},{7,15},{8,16},{9,17... | collective-permute-start | bytes 393224 | tf_op jit(solution)/shard_map/ppermute | solution.py:41
  43.5 12.7 %collective-permute-start.17 = (bf16[768,256]{1,0:T(8,128)(2,1)S(1)}, bf16[768,256]{1,0:T(8,128)(2,1)S(1)}, u32[]{:S(2)}, u32[]{:S(2)}) collective-permute-start(bf16[768,256]{1,0:T(8,128)(2,1)S(1)} %pad_maximum_fusion), channel_id=1, source_target_pairs={{0,192},{1,7},{2,194},{3,1},{4,196},{5,3},{6,198},{7,5},{8,200},{9... | collective-permute-start | bytes 1179656 | tf_op jit(solution)/shard_map/ppermute | solution.py:41
  45.6 13.5 %collective-permute-start.15 = (bf16[768,256]{1,0:T(8,128)(2,1)S(1)}, bf16[768,256]{1,0:T(8,128)(2,1)S(1)}, u32[]{:S(2)}, u32[]{:S(2)}) collective-permute-start(bf16[768,256]{1,0:T(8,128)(2,1)S(1)} %pad_maximum_fusion), channel_id=1, source_target_pairs={{0,64},{1,3},{2,66},{3,5},{4,68},{5,7},{6,70},{7,1},{8,72},{9,11},... | collective-permute-start | bytes 1179656 | tf_op jit(solution)/shard_map/ppermute | solution.py:41
  49.6 11.6 %collective-permute-start.19 = (bf16[1280,256]{1,0:T(8,128)(2,1)}, bf16[1280,256]{1,0:T(8,128)(2,1)S(1)}, u32[]{:S(2)}, u32[]{:S(2)}) collective-permute-start(bf16[1280,256]{1,0:T(8,128)(2,1)} %constant_dynamic-update-slice_fusion), channel_id=1, source_target_pairs={{0,192},{1,7},{2,194},{3,1},{4,196},{5,3},{6,198},{7,5},{8,200},{9... | collective-permute-start | bytes 1966088 | tf_op jit(solution)/shard_map/ppermute | solution.py:41
  49.6 20.6 %collective-permute-start.16 = (bf16[1280,256]{1,0:T(8,128)(2,1)}, bf16[1280,256]{1,0:T(8,128)(2,1)S(1)}, u32[]{:S(2)}, u32[]{:S(2)}) collective-permute-start(bf16[1280,256]{1,0:T(8,128)(2,1)} %collective-permute-done.14), channel_id=1, source_target_pairs={{0,64},{1,3},{2,66},{3,5},{4,68},{5,7},{6,70},{7,1},{8,72},{9,11},... | collective-permute-start | bytes 1966088 | tf_op jit(solution)/shard_map/ppermute | solution.py:41
  52.2 18.0 %collective-permute-start.11 = (bf16[16,128,128]{2,1,0:T(8,128)(2,1)S(1)}, bf16[16,128,128]{2,1,0:T(8,128)(2,1)S(1)}, u32[]{:S(2)}, u32[]{:S(2)}) collective-permute-start(bf16[16,128,128]{2,1,0:T(8,128)(2,1)S(1)} %slice.85), channel_id=1, source_target_pairs={{0,6},{1,193},{2,0},{3,195},{4,2},{5,197},{6,4},{7,199},{8,14},{9,... | collective-permute-start | bytes 1572872 | tf_op jit(solution)/shard_map/ppermute | solution.py:41
  56.1 15.3 %collective-permute-start.9 = (bf16[16,128,128]{2,1,0:T(8,128)(2,1)S(1)}, bf16[16,128,128]{2,1,0:T(8,128)(2,1)S(1)}, u32[]{:S(2)}, u32[]{:S(2)}) collective-permute-start(bf16[16,128,128]{2,1,0:T(8,128)(2,1)S(1)} %slice.84), channel_id=1, source_target_pairs={{0,2},{1,65},{2,4},{3,67},{4,6},{5,69},{6,0},{7,71},{8,10},{9,73},... | collective-permute-start | bytes 1572872 | tf_op jit(solution)/shard_map/ppermute | solution.py:41
  59.1 11.1 %collective-permute-start.18 = (bf16[768,256]{1,0:T(8,128)(2,1)S(1)}, bf16[768,256]{1,0:T(8,128)(2,1)S(1)}, u32[]{:S(2)}, u32[]{:S(2)}) collective-permute-start(bf16[768,256]{1,0:T(8,128)(2,1)S(1)} %collective-permute-done.17), channel_id=1, source_target_pairs={{0,192},{1,7},{2,194},{3,1},{4,196},{5,3},{6,198},{7,5},{8,200},{9... | collective-permute-start | bytes 1179656 | tf_op jit(solution)/shard_map/ppermute | solution.py:41
  78.2 4.0 %collective-permute-start.24 = (f32[32,256]{1,0:T(8,128)S(1)}, f32[32,256]{1,0:T(8,128)S(1)}, u32[]{:S(2)}, u32[]{:S(2)}) collective-permute-start(f32[32,256]{1,0:T(8,128)S(1)} %get-tuple-element.31), channel_id=1, source_target_pairs={{0,64},{1,3},{2,66},{3,5},{4,68},{5,7},{6,70},{7,1},{8,72},{9,11},... | collective-permute-start | bytes 98312 | tf_op jit(solution)/shard_map/ppermute | solution.py:41
  78.4 4.3 %collective-permute-start.23 = (f32[32,256]{1,0:T(8,128)S(1)}, f32[32,256]{1,0:T(8,128)S(1)}, u32[]{:S(2)}, u32[]{:S(2)}) collective-permute-start(f32[32,256]{1,0:T(8,128)S(1)} %get-tuple-element.31), channel_id=1, source_target_pairs={{0,128},{1,5},{2,130},{3,7},{4,132},{5,1},{6,134},{7,3},{8,136},{9... | collective-permute-start | bytes 98312 | tf_op jit(solution)/shard_map/ppermute | solution.py:41
  82.7 6.3 %collective-permute-start.28 = (f32[32,256]{1,0:T(8,128)S(1)}, f32[32,256]{1,0:T(8,128)S(1)}, u32[]{:S(2)}, u32[]{:S(2)}) collective-permute-start(f32[32,256]{1,0:T(8,128)S(1)} %add_add_fusion.1), channel_id=1, source_target_pairs={{0,48},{1,49},{2,50},{3,51},{4,52},{5,53},{6,54},{7,55},{8,56},{9,... | collective-permute-start | bytes 98312 | tf_op jit(solution)/shard_map/ppermute | solution.py:41
  83.9 6.3 %collective-permute-start.27 = (f32[32,256]{1,0:T(8,128)S(1)}, f32[32,256]{1,0:T(8,128)S(1)}, u32[]{:S(2)}, u32[]{:S(2)}) collective-permute-start(f32[32,256]{1,0:T(8,128)S(1)} %add_add_fusion.1), channel_id=1, source_target_pairs={{0,16},{1,17},{2,18},{3,19},{4,20},{5,21},{6,22},{7,23},{8,24},{9,... | collective-permute-start | bytes 98312 | tf_op jit(solution)/shard_map/ppermute | solution.py:41
  85.1 6.7 %collective-permute-start.26 = (f32[32,256]{1,0:T(8,128)S(1)}, f32[32,256]{1,0:T(8,128)S(1)}, u32[]{:S(2)}, u32[]{:S(2)}) collective-permute-start(f32[32,256]{1,0:T(8,128)S(1)} %add_add_fusion.1), channel_id=1, source_target_pairs={{0,32},{1,33},{2,34},{3,35},{4,36},{5,37},{6,38},{7,39},{8,40},{9,... | collective-permute-start | bytes 98312 | tf_op jit(solution)/shard_map/ppermute | solution.py:41
  87.0 16.8 %collective-permute-start.20 = (f32[128,256]{1,0:T(8,128)S(1)}, f32[128,256]{1,0:T(8,128)S(1)}, u32[]{:S(2)}, u32[]{:S(2)}) collective-permute-start(f32[128,256]{1,0:T(8,128)S(1)} %get-tuple-element.28), channel_id=1, source_target_pairs={{0,6},{1,193},{2,0},{3,195},{4,2},{5,197},{6,4},{7,199},{8,14},{9,... | collective-permute-start | bytes 393224 | tf_op jit(solution)/shard_map/ppermute | solution.py:41
  89.0 14.8 %collective-permute-start.21 = (f32[128,256]{1,0:T(8,128)S(1)}, f32[128,256]{1,0:T(8,128)S(1)}, u32[]{:S(2)}, u32[]{:S(2)}) collective-permute-start(f32[128,256]{1,0:T(8,128)S(1)} %get-tuple-element.29), channel_id=1, source_target_pairs={{0,2},{1,65},{2,4},{3,67},{4,6},{5,69},{6,0},{7,71},{8,10},{9,73},... | collective-permute-start | bytes 393224 | tf_op jit(solution)/shard_map/ppermute | solution.py:41
  89.0 14.8 %collective-permute-start.22 = (f32[128,256]{1,0:T(8,128)S(1)}, f32[128,256]{1,0:T(8,128)S(1)}, u32[]{:S(2)}, u32[]{:S(2)}) collective-permute-start(f32[128,256]{1,0:T(8,128)S(1)} %get-tuple-element.30), channel_id=1, source_target_pairs={{0,4},{1,129},{2,6},{3,131},{4,0},{5,133},{6,2},{7,135},{8,12},{9,... | collective-permute-start | bytes 393224 | tf_op jit(solution)/shard_map/ppermute | solution.py:41
  91.8 4.6 %collective-permute-start.29 = (f32[32,256]{1,0:T(8,128)S(1)}, f32[32,256]{1,0:T(8,128)S(1)}, u32[]{:S(2)}, u32[]{:S(2)}) collective-permute-start(f32[32,256]{1,0:T(8,128)S(1)} %add_add_fusion), channel_id=1, source_target_pairs={{0,8},{1,9},{2,10},{3,11},{4,12},{5,13},{6,14},{7,15},{8,16},{9,17... | collective-permute-start | bytes 98312 | tf_op jit(solution)/shard_map/ppermute | solution.py:41
  96.4 4.6 %collective-permute-start.32 = (f32[32,256]{1,0:T(8,128)S(1)}, f32[32,256]{1,0:T(8,128)S(1)}, u32[]{:S(2)}, u32[]{:S(2)}) collective-permute-start(f32[32,256]{1,0:T(8,128)S(1)} %add.92.refs_0_), channel_id=1, source_target_pairs={{0,4},{1,129},{2,6},{3,131},{4,0},{5,133},{6,2},{7,135},{8,12},{9,... | collective-permute-start | bytes 98312 | tf_op jit(solution)/shard_map/ppermute | solution.py:41
  97.6 4.8 %collective-permute-start.31 = (f32[32,256]{1,0:T(8,128)S(1)}, f32[32,256]{1,0:T(8,128)S(1)}, u32[]{:S(2)}, u32[]{:S(2)}) collective-permute-start(f32[32,256]{1,0:T(8,128)S(1)} %add.92.refs_0_), channel_id=1, source_target_pairs={{0,2},{1,65},{2,4},{3,67},{4,6},{5,69},{6,0},{7,71},{8,10},{9,73},... | collective-permute-start | bytes 98312 | tf_op jit(solution)/shard_map/ppermute | solution.py:41
  103.8 14.2 %collective-permute-start.33 = (f32[128,256]{1,0:T(8,128)S(1)}, f32[128,256]{1,0:T(8,128)S(1)}, u32[]{:S(2)}, u32[]{:S(2)}) collective-permute-start(f32[128,256]{1,0:T(8,128)S(1)} %get-tuple-element.32.refs_0_), channel_id=1, source_target_pairs={{0,1},{1,0},{2,3},{3,2},{4,5},{5,4},{6,7},{7,6},{8,9},{9,8},{10,11... | collective-permute-start | bytes 393224 | tf_op jit(solution)/shard_map/ppermute | solution.py:41
  114.0 4.1 %collective-permute-start.34 = (f32[128,256]{1,0:T(8,128)S(1)}, f32[128,256]{1,0:T(8,128)S(1)}, u32[]{:S(2)}, u32[]{:S(2)}) collective-permute-start(f32[128,256]{1,0:T(8,128)S(1)} %collective-permute-done.20.refs_1_), channel_id=1, source_target_pairs={{0,1},{1,0},{2,3},{3,2},{4,5},{5,4},{6,7},{7,6},{8,9},{9,8},{10,11... | collective-permute-start | bytes 393224 | tf_op jit(solution)/shard_map/ppermute | solution.py:41
  (14 other events, 113.8 us)

commit v2 on v1

--- a/solution.py
+++ b/solution.py
@@ -333,10 +333,11 @@
     pieces = [sums, send(sums, "u", -1), send(sums, "u", 1), send(sums, "u", 2)]
     owned, pieces = lax.optimization_barrier((owned, pieces))
     product = prompt(w_self, w_neigh, pieces)
-    prompt_grad = product + send(product, "rep", 0)
+    received = send(product, "rep", 0)
     other = [send(m, "rep", 0) for m in owned]
     input_grad = finish(self_term, w_neigh, owned, other)
-    return input_grad, prompt_grad
+    received, input_grad = lax.optimization_barrier((received, input_grad))
+    return input_grad, product + received
 
 
 def solution(mesh):

time: 121 us -> 120 us (level)
  starting transfers between devices: 54.8 us -> 53.4 us
    slice x0 -> x4, local copies, waits for them, and re-layouts: none -> 3.22 us  [shards(): own = jnp.concatenate([p[0:64] for p in packed], axis=0)]
    unnamed x23 -> x19, local copies, waits for them, and re-layouts: 6.8 us -> 3.58 us
    ppermute x38, starting transfers between devices: 54.8 us -> 53.4 us  [send(): return lax.ppermute(value, AXES, pairs_of(role, step))]
    ppermute x38, waiting for transfers between devices: 33.6 us -> 34.8 us  [send(): return lax.ppermute(value, AXES, pairs_of(role, step))]
  transfers between devices with their start and end apart: 38 -> 38, of which waited for: 14 -> 11; matrix products, arithmetic and copies ran while one was open for 14% -> 13% of each run, Pallas kernels for 2% -> 3%
where the time goes in v2:
time: 120 us
  starting transfers between devices  53.4 us (44%)
  waiting for transfers between devices  34.8 us (29%)
  local copies, waits for them, and re-layouts  15.6 us (13%)
  Pallas kernels  11.1 us (9%)
  other arithmetic  1.66 us (1%)
  matrix products  1.63 us (1%)
  between operations  1.49 us (1%)
    ppermute x38, starting transfers between devices, send(): return lax.ppermute(value, AXES, pairs_of(role, step))  53.4 us
    ppermute x38, waiting for transfers between devices, send(): return lax.ppermute(value, AXES, pairs_of(role, step))  34.8 us
    pallas_call x1, Pallas kernels, aggregate(): pl.pallas_call(aggregate_kernel, in_specs=[SMEM, VMEM] + [ANY] * 13, out_...  5.39 us
    unnamed x19, local copies, waits for them, and re-layouts  3.58 us
    slice x4, local copies, waits for them, and re-layouts, shards(): index = jnp.stack([p[64, 0:64] for p in packed]).astype(jnp.int32)  3.31 us
    slice x4, local copies, waits for them, and re-layouts, shards(): own = jnp.concatenate([p[0:64] for p in packed], axis=0)  3.22 us
    slice x4, local copies, waits for them, and re-layouts, shards(): ids = jnp.stack([p[64, 128:256] for p in packed]).astype(jnp.int32)  2.7 us
  transfers between devices with their start and end apart: 38, of which 11 were waited for; matrix products, arithmetic and copies ran while one was open for 13% of the time, Pallas kernels for 3%

profile of v2, /device:TPU:1, one launch (start us, length us, event | category | flops | bytes accessed | tf_op | source)
XLA Modules:
  0.0 119.7 jit_solution(1406760161432912864)
XLA Ops:
  1.3 1.7 %split.1 = (bf16[80,256]{1,0:T(8,128)(2,1)}, bf16[80,256]{1,0:T(8,128)(2,1)}, bf16[80,256]{1,0:T(8,128)(2,1)}, bf16[80,256]{1,0:T(8,128)(2,1)}) custom-call(s32[1]{0:T(128)S(6)} %copy.16.count, s32[1,64]{1,0:T(1,128)} %index.1, s32[1,128]{1,0:T(1,128)} %bitcast.19, bf16[128,1024]{1,0:T(8,128)(2,1)} %grad.1), custom_call_target="tpu_custom_call" | custom-call | tf_op jit(solution)/shard_map/split/pallas_call | solution.py:124
  2.9 2.1 %collective-permute-start = (bf16[80,256]{1,0:T(8,128)(2,1)}, bf16[80,256]{1,0:T(8,128)(2,1)S(1)}, u32[]{:S(2)}, u32[]{:S(2)}) collective-permute-start(bf16[80,256]{1,0:T(8,128)(2,1)} %get-tuple-element.24), channel_id=1, source_target_pairs={{0,2},{1,65},{2,4},{3,67},{4,6},{5,69},{6,0},{7,71},{8,10},{9,73},... | collective-permute-start | bytes 122888 | tf_op jit(solution)/shard_map/ppermute | solution.py:41
  5.1 2.6 %collective-permute-start.1 = (bf16[80,256]{1,0:T(8,128)(2,1)}, bf16[80,256]{1,0:T(8,128)(2,1)S(1)}, u32[]{:S(2)}, u32[]{:S(2)}) collective-permute-start(bf16[80,256]{1,0:T(8,128)(2,1)} %get-tuple-element.25), channel_id=1, source_target_pairs={{0,4},{1,129},{2,6},{3,131},{4,0},{5,133},{6,2},{7,135},{8,12},{9,... | collective-permute-start | bytes 122888 | tf_op jit(solution)/shard_map/ppermute | solution.py:41
  8.8 1.4 %fusion.12 = (bf16[64,256]{1,0:T(8,128)(2,1)S(1)}, bf16[1280,256]{1,0:T(8,128)(2,1)}) fusion(bf16[80,256]{1,0:T(8,128)(2,1)} %get-tuple-element.23), kind=kLoop, calls=%fused_computation.49 | loop fusion | bytes 98304 | tf_op jit(solution)/shard_map/slice | solution.py:290
  12.0 6.1 %collective-permute-start.10 = (bf16[256,256]{1,0:T(8,128)(2,1)S(1)}, bf16[256,256]{1,0:T(8,128)(2,1)S(1)}, u32[]{:S(2)}, u32[]{:S(2)}) collective-permute-start(bf16[256,256]{1,0:T(8,128)(2,1)S(1)} %pad_maximum_fusion.1), channel_id=1, source_target_pairs={{0,48},{1,49},{2,50},{3,51},{4,52},{5,53},{6,54},{7,55},{8,56},{9,... | collective-permute-start | bytes 393224 | tf_op jit(solution)/shard_map/ppermute | solution.py:41
  18.8 1.9 %collective-permute-start.8 = (bf16[256,256]{1,0:T(8,128)(2,1)S(1)}, bf16[256,256]{1,0:T(8,128)(2,1)S(1)}, u32[]{:S(2)}, u32[]{:S(2)}) collective-permute-start(bf16[256,256]{1,0:T(8,128)(2,1)S(1)} %pad_maximum_fusion.1), channel_id=1, source_target_pairs={{0,56},{1,57},{2,58},{3,59},{4,60},{5,61},{6,62},{7,63},{8,0},{9,1... | collective-permute-start | bytes 393224 | tf_op jit(solution)/shard_map/ppermute | solution.py:41
  20.8 1.6 %copy-done.2 = bf16[1,64,128,128]{3,2,1,0:T(8,128)(2,1)S(1)} copy-done((bf16[1,64,128,128]{3,2,1,0:T(8,128)(2,1)S(1)}, bf16[1,64,128,128]{3,2,1,0:T(8,128)(2,1)}, u32[]{:S(2)}) %copy-start.2) | copy-done | bytes 2097176
  23.3 1.7 %collective-permute-start.5 = (bf16[32,128,128]{2,1,0:T(8,128)(2,1)S(1)}, bf16[32,128,128]{2,1,0:T(8,128)(2,1)}, u32[]{:S(2)}, u32[]{:S(2)}) collective-permute-start(bf16[32,128,128]{2,1,0:T(8,128)(2,1)S(1)} %pack.1.refs_0_), channel_id=1, source_target_pairs={{0,6},{1,193},{2,0},{3,195},{4,2},{5,197},{6,4},{7,199},{8,14},{9,... | collective-permute-start | bytes 3145736 | tf_op jit(solution)/shard_map/ppermute | solution.py:41
  25.0 1.9 %collective-permute-start.13 = (bf16[256,256]{1,0:T(8,128)(2,1)S(1)}, bf16[256,256]{1,0:T(8,128)(2,1)S(1)}, u32[]{:S(2)}, u32[]{:S(2)}) collective-permute-start(bf16[256,256]{1,0:T(8,128)(2,1)S(1)} %collective-permute-done.10), channel_id=1, source_target_pairs={{0,56},{1,57},{2,58},{3,59},{4,60},{5,61},{6,62},{7,63},{8,0},{9,1... | collective-permute-start | bytes 393224 | tf_op jit(solution)/shard_map/ppermute | solution.py:41
  28.2 5.0 %collective-permute-done.9 = bf16[256,256]{1,0:T(8,128)(2,1)S(1)} collective-permute-done((bf16[256,256]{1,0:T(8,128)(2,1)S(1)}, bf16[256,256]{1,0:T(8,128)(2,1)S(1)}, u32[]{:S(2)}, u32[]{:S(2)}) %collective-permute-start.9) | collective-permute-done | bytes 131104 | tf_op jit(solution)/shard_map/ppermute | solution.py:41
  34.6 1.8 %collective-permute-start.14 = (bf16[1280,256]{1,0:T(8,128)(2,1)}, bf16[1280,256]{1,0:T(8,128)(2,1)}, u32[]{:S(2)}, u32[]{:S(2)}) collective-permute-start(bf16[1280,256]{1,0:T(8,128)(2,1)} %constant_dynamic-update-slice_fusion), channel_id=1, source_target_pairs={{0,64},{1,3},{2,66},{3,5},{4,68},{5,7},{6,70},{7,1},{8,72},{9,11},... | collective-permute-start | bytes 1966088 | tf_op jit(solution)/shard_map/ppermute | solution.py:41
  36.5 1.6 %fusion.20.self_term = f32[128,1024]{1,0:T(8,128)} fusion(bf16[128,1024]{1,0:T(8,128)(2,1)S(1)} %copy-done.4, bf16[1024,1024]{1,0:T(8,128)(2,1)S(1)} %copy-done), kind=kOutput, calls=%fused_computation.57 | convolution fusion | flops 268435456 | bytes 2883584 | tf_op jit(solution)/shard_map/dot_general | solution.py:225
  38.8 4.6 %collective-permute-done.12 = bf16[256,256]{1,0:T(8,128)(2,1)S(1)} collective-permute-done((bf16[256,256]{1,0:T(8,128)(2,1)S(1)}, bf16[256,256]{1,0:T(8,128)(2,1)S(1)}, u32[]{:S(2)}, u32[]{:S(2)}) %collective-permute-start.12) | collective-permute-done | bytes 131104 | tf_op jit(solution)/shard_map/ppermute | solution.py:41
  45.8 2.1 %collective-permute-start.15 = (bf16[768,256]{1,0:T(8,128)(2,1)S(1)}, bf16[768,256]{1,0:T(8,128)(2,1)S(1)}, u32[]{:S(2)}, u32[]{:S(2)}) collective-permute-start(bf16[768,256]{1,0:T(8,128)(2,1)S(1)} %pad_maximum_fusion), channel_id=1, source_target_pairs={{0,64},{1,3},{2,66},{3,5},{4,68},{5,7},{6,70},{7,1},{8,72},{9,11},... | collective-permute-start | bytes 1179656 | tf_op jit(solution)/shard_map/ppermute | solution.py:41
  48.7 2.1 %collective-permute-done.14 = bf16[1280,256]{1,0:T(8,128)(2,1)} collective-permute-done((bf16[1280,256]{1,0:T(8,128)(2,1)}, bf16[1280,256]{1,0:T(8,128)(2,1)}, u32[]{:S(2)}, u32[]{:S(2)}) %collective-permute-start.14) | collective-permute-done | bytes 655392 | tf_op jit(solution)/shard_map/ppermute | solution.py:41
  50.8 1.5 %collective-permute-start.16 = (bf16[1280,256]{1,0:T(8,128)(2,1)}, bf16[1280,256]{1,0:T(8,128)(2,1)S(1)}, u32[]{:S(2)}, u32[]{:S(2)}) collective-permute-start(bf16[1280,256]{1,0:T(8,128)(2,1)} %collective-permute-done.14), channel_id=1, source_target_pairs={{0,64},{1,3},{2,66},{3,5},{4,68},{5,7},{6,70},{7,1},{8,72},{9,11},... | collective-permute-start | bytes 1966088 | tf_op jit(solution)/shard_map/ppermute | solution.py:41
  53.4 3.0 %collective-permute-start.6 = (bf16[16,128,128]{2,1,0:T(8,128)(2,1)S(1)}, bf16[16,128,128]{2,1,0:T(8,128)(2,1)S(1)}, u32[]{:S(2)}, u32[]{:S(2)}) collective-permute-start(bf16[16,128,128]{2,1,0:T(8,128)(2,1)S(1)} %slice.82), channel_id=1, source_target_pairs={{0,6},{1,193},{2,0},{3,195},{4,2},{5,197},{6,4},{7,199},{8,14},{9,... | collective-permute-start | bytes 1572872 | tf_op jit(solution)/shard_map/ppermute | solution.py:41
  60.3 2.4 %collective-permute-start.18 = (bf16[768,256]{1,0:T(8,128)(2,1)S(1)}, bf16[768,256]{1,0:T(8,128)(2,1)S(1)}, u32[]{:S(2)}, u32[]{:S(2)}) collective-permute-start(bf16[768,256]{1,0:T(8,128)(2,1)S(1)} %collective-permute-done.17), channel_id=1, source_target_pairs={{0,192},{1,7},{2,194},{3,1},{4,196},{5,3},{6,198},{7,5},{8,200},{9... | collective-permute-start | bytes 1179656 | tf_op jit(solution)/shard_map/ppermute | solution.py:41
  63.7 7.8 %collective-permute-done.18 = bf16[768,256]{1,0:T(8,128)(2,1)S(1)} collective-permute-done((bf16[768,256]{1,0:T(8,128)(2,1)S(1)}, bf16[768,256]{1,0:T(8,128)(2,1)S(1)}, u32[]{:S(2)}, u32[]{:S(2)}) %collective-permute-start.18) | collective-permute-done | bytes 393248 | tf_op jit(solution)/shard_map/ppermute | solution.py:41
  72.7 5.4 %aggregate.1 = (f32[128,256]{1,0:T(8,128)S(1)}, f32[128,256]{1,0:T(8,128)S(1)}, f32[128,256]{1,0:T(8,128)S(1)}, f32[128,256]{1,0:T(8,128)S(1)}, f32[32,256]{1,0:T(8,128)S(1)}) custom-call(s32[4,64]{1,0:T(4,128)S(1)} %fusion.5.where, s32[4,128]{1,0:T(4,128)S(1)} %maximum_convert_fusion.ids, bf16[32,128,128]{2,1,0:T(8,128)(2,1)S(1)} %pack.1.refs_0_, ...), custom_call_target="tpu_custom_call" | custom-call | tf_op jit(solution)/shard_map/aggregate/pallas_call | solution.py:187
  78.1 2.2 %collective-permute-start.25 = (f32[32,256]{1,0:T(8,128)S(1)}, f32[32,256]{1,0:T(8,128)S(1)}, u32[]{:S(2)}, u32[]{:S(2)}) collective-permute-start(f32[32,256]{1,0:T(8,128)S(1)} %get-tuple-element.32), channel_id=1, source_target_pairs={{0,192},{1,7},{2,194},{3,1},{4,196},{5,3},{6,198},{7,5},{8,200},{9... | collective-permute-start | bytes 98312 | tf_op jit(solution)/shard_map/ppermute | solution.py:41
  81.6 2.7 %collective-permute-done.24 = f32[32,256]{1,0:T(8,128)S(1)} collective-permute-done((f32[32,256]{1,0:T(8,128)S(1)}, f32[32,256]{1,0:T(8,128)S(1)}, u32[]{:S(2)}, u32[]{:S(2)}) %collective-permute-start.24) | collective-permute-done | bytes 32800 | tf_op jit(solution)/shard_map/ppermute | solution.py:41
  85.4 1.7 %collective-permute-start.27 = (f32[32,256]{1,0:T(8,128)S(1)}, f32[32,256]{1,0:T(8,128)S(1)}, u32[]{:S(2)}, u32[]{:S(2)}) collective-permute-start(f32[32,256]{1,0:T(8,128)S(1)} %add_add_fusion.1), channel_id=1, source_target_pairs={{0,16},{1,17},{2,18},{3,19},{4,20},{5,21},{6,22},{7,23},{8,24},{9,... | collective-permute-start | bytes 98312 | tf_op jit(solution)/shard_map/ppermute | solution.py:41
  87.6 1.6 %collective-permute-start.20 = (f32[128,256]{1,0:T(8,128)S(1)}, f32[128,256]{1,0:T(8,128)S(1)}, u32[]{:S(2)}, u32[]{:S(2)}) collective-permute-start(f32[128,256]{1,0:T(8,128)S(1)} %get-tuple-element.29), channel_id=1, source_target_pairs={{0,6},{1,193},{2,0},{3,195},{4,2},{5,197},{6,4},{7,199},{8,14},{9,... | collective-permute-start | bytes 393224 | tf_op jit(solution)/shard_map/ppermute | solution.py:41
  90.4 3.7 %collective-permute-done.26 = f32[32,256]{1,0:T(8,128)S(1)} collective-permute-done((f32[32,256]{1,0:T(8,128)S(1)}, f32[32,256]{1,0:T(8,128)S(1)}, u32[]{:S(2)}, u32[]{:S(2)}) %collective-permute-start.26) | collective-permute-done | bytes 32800 | tf_op jit(solution)/shard_map/ppermute | solution.py:41
  94.4 4.0 %collective-permute-done.29 = f32[32,256]{1,0:T(8,128)S(1)} collective-permute-done((f32[32,256]{1,0:T(8,128)S(1)}, f32[32,256]{1,0:T(8,128)S(1)}, u32[]{:S(2)}, u32[]{:S(2)}) %collective-permute-start.29) | collective-permute-done | bytes 32800 | tf_op jit(solution)/shard_map/ppermute | solution.py:41
  98.5 2.2 %collective-permute-start.31 = (f32[32,256]{1,0:T(8,128)S(1)}, f32[32,256]{1,0:T(8,128)S(1)}, u32[]{:S(2)}, u32[]{:S(2)}) collective-permute-start(f32[32,256]{1,0:T(8,128)S(1)} %add.92.refs_0_), channel_id=1, source_target_pairs={{0,2},{1,65},{2,4},{3,67},{4,6},{5,69},{6,0},{7,71},{8,10},{9,73},... | collective-permute-start | bytes 98312 | tf_op jit(solution)/shard_map/ppermute | solution.py:41
  100.6 2.2 %collective-permute-done.32.refs_3_ = f32[32,256]{1,0:T(8,128)S(1)} collective-permute-done((f32[32,256]{1,0:T(8,128)S(1)}, f32[32,256]{1,0:T(8,128)S(1)}, u32[]{:S(2)}, u32[]{:S(2)}) %collective-permute-start.32) | collective-permute-done | bytes 32800 | tf_op jit(solution)/shard_map/ppermute | solution.py:41
  102.8 1.8 %collective-permute-start.30 = (f32[32,256]{1,0:T(8,128)S(1)}, f32[32,256]{1,0:T(8,128)S(1)}, u32[]{:S(2)}, u32[]{:S(2)}) collective-permute-start(f32[32,256]{1,0:T(8,128)S(1)} %add.92.refs_0_), channel_id=1, source_target_pairs={{0,6},{1,193},{2,0},{3,195},{4,2},{5,197},{6,4},{7,199},{8,14},{9,... | collective-permute-start | bytes 98312 | tf_op jit(solution)/shard_map/ppermute | solution.py:41
  105.7 9.1 %collective-permute-start.34 = (f32[128,256]{1,0:T(8,128)S(1)}, f32[128,256]{1,0:T(8,128)S(1)}, u32[]{:S(2)}, u32[]{:S(2)}) collective-permute-start(f32[128,256]{1,0:T(8,128)S(1)} %get-tuple-element.38.refs_0_), channel_id=1, source_target_pairs={{0,1},{1,0},{2,3},{3,2},{4,5},{5,4},{6,7},{7,6},{8,9},{9,8},{10,11... | collective-permute-start | bytes 393224 | tf_op jit(solution)/shard_map/ppermute | solution.py:41
  115.4 1.4 %prompt.1 = f32[16,1024]{1,0:T(8,128)S(1)} custom-call(bf16[1024,1024]{1,0:T(8,128)(2,1)S(1)} %copy-done, bf16[1024,1024]{1,0:T(8,128)(2,1)S(1)} %copy-done.1, f32[32,256]{1,0:T(8,128)S(1)} %add.92.refs_0_, f32[32,256]{1,0:T(8,128)S(1)} %collective-permute-done.30.refs_1_, f32[32,256]{1,0:T(8,128)S(1)} %collective-permute-done.31.refs_2_, ...), custom_call_target="tpu_custom_call" | custom-call | tf_op jit(solution)/shard_map/prompt/pallas_call | solution.py:268
  117.3 1.8 %finish.1 = bf16[128,1024]{1,0:T(8,128)(2,1)} custom-call(f32[128,1024]{1,0:T(8,128)S(1)} %copy-done.3, bf16[1024,1024]{1,0:T(8,128)(2,1)S(1)} %copy-done.1, f32[128,256]{1,0:T(8,128)S(1)} %get-tuple-element.38.refs_0_, f32[128,256]{1,0:T(8,128)S(1)} %collective-permute-done.20.refs_1_, f32[128,256]{1,0:T(8,128)S(1)} %collective-permute-done.21.refs_2_, ...), custom_call_target="tpu_custom_call" | custom-call | tf_op jit(solution)/shard_map/finish/pallas_call | solution.py:236
  (92 shorter events, 25.6 us)
Async XLA Ops:
  2.9 7.2 %collective-permute-start = (bf16[80,256]{1,0:T(8,128)(2,1)}, bf16[80,256]{1,0:T(8,128)(2,1)S(1)}, u32[]{:S(2)}, u32[]{:S(2)}) collective-permute-start(bf16[80,256]{1,0:T(8,128)(2,1)} %get-tuple-element.24), channel_id=1, source_target_pairs={{0,2},{1,65},{2,4},{3,67},{4,6},{5,69},{6,0},{7,71},{8,10},{9,73},... | collective-permute-start | bytes 122888 | tf_op jit(solution)/shard_map/ppermute | solution.py:41
  5.1 5.7 %collective-permute-start.1 = (bf16[80,256]{1,0:T(8,128)(2,1)}, bf16[80,256]{1,0:T(8,128)(2,1)S(1)}, u32[]{:S(2)}, u32[]{:S(2)}) collective-permute-start(bf16[80,256]{1,0:T(8,128)(2,1)} %get-tuple-element.25), channel_id=1, source_target_pairs={{0,4},{1,129},{2,6},{3,131},{4,0},{5,133},{6,2},{7,135},{8,12},{9,... | collective-permute-start | bytes 122888 | tf_op jit(solution)/shard_map/ppermute | solution.py:41
  7.7 3.7 %collective-permute-start.2 = (bf16[80,256]{1,0:T(8,128)(2,1)}, bf16[80,256]{1,0:T(8,128)(2,1)S(1)}, u32[]{:S(2)}, u32[]{:S(2)}) collective-permute-start(bf16[80,256]{1,0:T(8,128)(2,1)} %get-tuple-element.26), channel_id=1, source_target_pairs={{0,6},{1,193},{2,0},{3,195},{4,2},{5,197},{6,4},{7,199},{8,14},{9,... | collective-permute-start | bytes 122888 | tf_op jit(solution)/shard_map/ppermute | solution.py:41
  12.0 13.0 %collective-permute-start.10 = (bf16[256,256]{1,0:T(8,128)(2,1)S(1)}, bf16[256,256]{1,0:T(8,128)(2,1)S(1)}, u32[]{:S(2)}, u32[]{:S(2)}) collective-permute-start(bf16[256,256]{1,0:T(8,128)(2,1)S(1)} %pad_maximum_fusion.1), channel_id=1, source_target_pairs={{0,48},{1,49},{2,50},{3,51},{4,52},{5,53},{6,54},{7,55},{8,56},{9,... | collective-permute-start | bytes 393224 | tf_op jit(solution)/shard_map/ppermute | solution.py:41
  18.1 6.9 %collective-permute-start.7 = (bf16[256,256]{1,0:T(8,128)(2,1)S(1)}, bf16[256,256]{1,0:T(8,128)(2,1)S(1)}, u32[]{:S(2)}, u32[]{:S(2)}) collective-permute-start(bf16[256,256]{1,0:T(8,128)(2,1)S(1)} %pad_maximum_fusion.1), channel_id=1, source_target_pairs={{0,8},{1,9},{2,10},{3,11},{4,12},{5,13},{6,14},{7,15},{8,16},{9,17... | collective-permute-start | bytes 393224 | tf_op jit(solution)/shard_map/ppermute | solution.py:41
  18.8 8.8 %collective-permute-start.8 = (bf16[256,256]{1,0:T(8,128)(2,1)S(1)}, bf16[256,256]{1,0:T(8,128)(2,1)S(1)}, u32[]{:S(2)}, u32[]{:S(2)}) collective-permute-start(bf16[256,256]{1,0:T(8,128)(2,1)S(1)} %pad_maximum_fusion.1), channel_id=1, source_target_pairs={{0,56},{1,57},{2,58},{3,59},{4,60},{5,61},{6,62},{7,63},{8,0},{9,1... | collective-permute-start | bytes 393224 | tf_op jit(solution)/shard_map/ppermute | solution.py:41
  23.3 27.5 %collective-permute-start.5 = (bf16[32,128,128]{2,1,0:T(8,128)(2,1)S(1)}, bf16[32,128,128]{2,1,0:T(8,128)(2,1)}, u32[]{:S(2)}, u32[]{:S(2)}) collective-permute-start(bf16[32,128,128]{2,1,0:T(8,128)(2,1)S(1)} %pack.1.refs_0_), channel_id=1, source_target_pairs={{0,6},{1,193},{2,0},{3,195},{4,2},{5,197},{6,4},{7,199},{8,14},{9,... | collective-permute-start | bytes 3145736 | tf_op jit(solution)/shard_map/ppermute | solution.py:41
  25.0 28.3 %collective-permute-start.3 = (bf16[32,128,128]{2,1,0:T(8,128)(2,1)S(1)}, bf16[32,128,128]{2,1,0:T(8,128)(2,1)}, u32[]{:S(2)}, u32[]{:S(2)}) collective-permute-start(bf16[32,128,128]{2,1,0:T(8,128)(2,1)S(1)} %pack.1.refs_0_), channel_id=1, source_target_pairs={{0,2},{1,65},{2,4},{3,67},{4,6},{5,69},{6,0},{7,71},{8,10},{9,73},... | collective-permute-start | bytes 3145736 | tf_op jit(solution)/shard_map/ppermute | solution.py:41
  25.0 8.2 %collective-permute-start.9 = (bf16[256,256]{1,0:T(8,128)(2,1)S(1)}, bf16[256,256]{1,0:T(8,128)(2,1)S(1)}, u32[]{:S(2)}, u32[]{:S(2)}) collective-permute-start(bf16[256,256]{1,0:T(8,128)(2,1)S(1)} %pad_maximum_fusion.1), channel_id=1, source_target_pairs={{0,16},{1,17},{2,18},{3,19},{4,20},{5,21},{6,22},{7,23},{8,24},{9,... | collective-permute-start | bytes 393224 | tf_op jit(solution)/shard_map/ppermute | solution.py:41
  25.0 11.4 %collective-permute-start.13 = (bf16[256,256]{1,0:T(8,128)(2,1)S(1)}, bf16[256,256]{1,0:T(8,128)(2,1)S(1)}, u32[]{:S(2)}, u32[]{:S(2)}) collective-permute-start(bf16[256,256]{1,0:T(8,128)(2,1)S(1)} %collective-permute-done.10), channel_id=1, source_target_pairs={{0,56},{1,57},{2,58},{3,59},{4,60},{5,61},{6,62},{7,63},{8,0},{9,1... | collective-permute-start | bytes 393224 | tf_op jit(solution)/shard_map/ppermute | solution.py:41
  34.6 16.2 %collective-permute-start.14 = (bf16[1280,256]{1,0:T(8,128)(2,1)}, bf16[1280,256]{1,0:T(8,128)(2,1)}, u32[]{:S(2)}, u32[]{:S(2)}) collective-permute-start(bf16[1280,256]{1,0:T(8,128)(2,1)} %constant_dynamic-update-slice_fusion), channel_id=1, source_target_pairs={{0,64},{1,3},{2,66},{3,5},{4,68},{5,7},{6,70},{7,1},{8,72},{9,11},... | collective-permute-start | bytes 1966088 | tf_op jit(solution)/shard_map/ppermute | solution.py:41
  36.4 7.0 %collective-permute-start.12 = (bf16[256,256]{1,0:T(8,128)(2,1)S(1)}, bf16[256,256]{1,0:T(8,128)(2,1)S(1)}, u32[]{:S(2)}, u32[]{:S(2)}) collective-permute-start(bf16[256,256]{1,0:T(8,128)(2,1)S(1)} %collective-permute-done.9), channel_id=1, source_target_pairs={{0,16},{1,17},{2,18},{3,19},{4,20},{5,21},{6,22},{7,23},{8,24},{9,... | collective-permute-start | bytes 393224 | tf_op jit(solution)/shard_map/ppermute | solution.py:41
  36.4 7.0 %collective-permute-start.11 = (bf16[256,256]{1,0:T(8,128)(2,1)S(1)}, bf16[256,256]{1,0:T(8,128)(2,1)}, u32[]{:S(2)}, u32[]{:S(2)}) collective-permute-start(bf16[256,256]{1,0:T(8,128)(2,1)S(1)} %collective-permute-done.9), channel_id=1, source_target_pairs={{0,8},{1,9},{2,10},{3,11},{4,12},{5,13},{6,14},{7,15},{8,16},{9,17... | collective-permute-start | bytes 393224 | tf_op jit(solution)/shard_map/ppermute | solution.py:41
  44.3 13.1 %collective-permute-start.17 = (bf16[768,256]{1,0:T(8,128)(2,1)S(1)}, bf16[768,256]{1,0:T(8,128)(2,1)S(1)}, u32[]{:S(2)}, u32[]{:S(2)}) collective-permute-start(bf16[768,256]{1,0:T(8,128)(2,1)S(1)} %pad_maximum_fusion), channel_id=1, source_target_pairs={{0,192},{1,7},{2,194},{3,1},{4,196},{5,3},{6,198},{7,5},{8,200},{9... | collective-permute-start | bytes 1179656 | tf_op jit(solution)/shard_map/ppermute | solution.py:41
  45.8 14.5 %collective-permute-start.15 = (bf16[768,256]{1,0:T(8,128)(2,1)S(1)}, bf16[768,256]{1,0:T(8,128)(2,1)S(1)}, u32[]{:S(2)}, u32[]{:S(2)}) collective-permute-start(bf16[768,256]{1,0:T(8,128)(2,1)S(1)} %pad_maximum_fusion), channel_id=1, source_target_pairs={{0,64},{1,3},{2,66},{3,5},{4,68},{5,7},{6,70},{7,1},{8,72},{9,11},... | collective-permute-start | bytes 1179656 | tf_op jit(solution)/shard_map/ppermute | solution.py:41
  50.8 12.9 %collective-permute-start.19 = (bf16[1280,256]{1,0:T(8,128)(2,1)}, bf16[1280,256]{1,0:T(8,128)(2,1)S(1)}, u32[]{:S(2)}, u32[]{:S(2)}) collective-permute-start(bf16[1280,256]{1,0:T(8,128)(2,1)} %constant_dynamic-update-slice_fusion), channel_id=1, source_target_pairs={{0,192},{1,7},{2,194},{3,1},{4,196},{5,3},{6,198},{7,5},{8,200},{9... | collective-permute-start | bytes 1966088 | tf_op jit(solution)/shard_map/ppermute | solution.py:41
  50.8 20.6 %collective-permute-start.16 = (bf16[1280,256]{1,0:T(8,128)(2,1)}, bf16[1280,256]{1,0:T(8,128)(2,1)S(1)}, u32[]{:S(2)}, u32[]{:S(2)}) collective-permute-start(bf16[1280,256]{1,0:T(8,128)(2,1)} %collective-permute-done.14), channel_id=1, source_target_pairs={{0,64},{1,3},{2,66},{3,5},{4,68},{5,7},{6,70},{7,1},{8,72},{9,11},... | collective-permute-start | bytes 1966088 | tf_op jit(solution)/shard_map/ppermute | solution.py:41
  53.4 18.1 %collective-permute-start.6 = (bf16[16,128,128]{2,1,0:T(8,128)(2,1)S(1)}, bf16[16,128,128]{2,1,0:T(8,128)(2,1)S(1)}, u32[]{:S(2)}, u32[]{:S(2)}) collective-permute-start(bf16[16,128,128]{2,1,0:T(8,128)(2,1)S(1)} %slice.82), channel_id=1, source_target_pairs={{0,6},{1,193},{2,0},{3,195},{4,2},{5,197},{6,4},{7,199},{8,14},{9,... | collective-permute-start | bytes 1572872 | tf_op jit(solution)/shard_map/ppermute | solution.py:41
  57.4 15.3 %collective-permute-start.4 = (bf16[16,128,128]{2,1,0:T(8,128)(2,1)S(1)}, bf16[16,128,128]{2,1,0:T(8,128)(2,1)S(1)}, u32[]{:S(2)}, u32[]{:S(2)}) collective-permute-start(bf16[16,128,128]{2,1,0:T(8,128)(2,1)S(1)} %slice.81), channel_id=1, source_target_pairs={{0,2},{1,65},{2,4},{3,67},{4,6},{5,69},{6,0},{7,71},{8,10},{9,73},... | collective-permute-start | bytes 1572872 | tf_op jit(solution)/shard_map/ppermute | solution.py:41
  60.3 11.1 %collective-permute-start.18 = (bf16[768,256]{1,0:T(8,128)(2,1)S(1)}, bf16[768,256]{1,0:T(8,128)(2,1)S(1)}, u32[]{:S(2)}, u32[]{:S(2)}) collective-permute-start(bf16[768,256]{1,0:T(8,128)(2,1)S(1)} %collective-permute-done.17), channel_id=1, source_target_pairs={{0,192},{1,7},{2,194},{3,1},{4,196},{5,3},{6,198},{7,5},{8,200},{9... | collective-permute-start | bytes 1179656 | tf_op jit(solution)/shard_map/ppermute | solution.py:41
  80.3 4.0 %collective-permute-start.24 = (f32[32,256]{1,0:T(8,128)S(1)}, f32[32,256]{1,0:T(8,128)S(1)}, u32[]{:S(2)}, u32[]{:S(2)}) collective-permute-start(f32[32,256]{1,0:T(8,128)S(1)} %get-tuple-element.32), channel_id=1, source_target_pairs={{0,64},{1,3},{2,66},{3,5},{4,68},{5,7},{6,70},{7,1},{8,72},{9,11},... | collective-permute-start | bytes 98312 | tf_op jit(solution)/shard_map/ppermute | solution.py:41
  80.3 4.3 %collective-permute-start.23 = (f32[32,256]{1,0:T(8,128)S(1)}, f32[32,256]{1,0:T(8,128)S(1)}, u32[]{:S(2)}, u32[]{:S(2)}) collective-permute-start(f32[32,256]{1,0:T(8,128)S(1)} %get-tuple-element.32), channel_id=1, source_target_pairs={{0,128},{1,5},{2,130},{3,7},{4,132},{5,1},{6,134},{7,3},{8,136},{9... | collective-permute-start | bytes 98312 | tf_op jit(solution)/shard_map/ppermute | solution.py:41
  84.7 4.5 %collective-permute-start.28 = (f32[32,256]{1,0:T(8,128)S(1)}, f32[32,256]{1,0:T(8,128)S(1)}, u32[]{:S(2)}, u32[]{:S(2)}) collective-permute-start(f32[32,256]{1,0:T(8,128)S(1)} %add_add_fusion.1), channel_id=1, source_target_pairs={{0,48},{1,49},{2,50},{3,51},{4,52},{5,53},{6,54},{7,55},{8,56},{9,... | collective-permute-start | bytes 98312 | tf_op jit(solution)/shard_map/ppermute | solution.py:41
  85.4 4.9 %collective-permute-start.27 = (f32[32,256]{1,0:T(8,128)S(1)}, f32[32,256]{1,0:T(8,128)S(1)}, u32[]{:S(2)}, u32[]{:S(2)}) collective-permute-start(f32[32,256]{1,0:T(8,128)S(1)} %add_add_fusion.1), channel_id=1, source_target_pairs={{0,16},{1,17},{2,18},{3,19},{4,20},{5,21},{6,22},{7,23},{8,24},{9,... | collective-permute-start | bytes 98312 | tf_op jit(solution)/shard_map/ppermute | solution.py:41
  87.1 6.9 %collective-permute-start.26 = (f32[32,256]{1,0:T(8,128)S(1)}, f32[32,256]{1,0:T(8,128)S(1)}, u32[]{:S(2)}, u32[]{:S(2)}) collective-permute-start(f32[32,256]{1,0:T(8,128)S(1)} %add_add_fusion.1), channel_id=1, source_target_pairs={{0,32},{1,33},{2,34},{3,35},{4,36},{5,37},{6,38},{7,39},{8,40},{9,... | collective-permute-start | bytes 98312 | tf_op jit(solution)/shard_map/ppermute | solution.py:41
  87.6 18.1 %collective-permute-start.20 = (f32[128,256]{1,0:T(8,128)S(1)}, f32[128,256]{1,0:T(8,128)S(1)}, u32[]{:S(2)}, u32[]{:S(2)}) collective-permute-start(f32[128,256]{1,0:T(8,128)S(1)} %get-tuple-element.29), channel_id=1, source_target_pairs={{0,6},{1,193},{2,0},{3,195},{4,2},{5,197},{6,4},{7,199},{8,14},{9,... | collective-permute-start | bytes 393224 | tf_op jit(solution)/shard_map/ppermute | solution.py:41
  89.2 16.5 %collective-permute-start.21 = (f32[128,256]{1,0:T(8,128)S(1)}, f32[128,256]{1,0:T(8,128)S(1)}, u32[]{:S(2)}, u32[]{:S(2)}) collective-permute-start(f32[128,256]{1,0:T(8,128)S(1)} %get-tuple-element.30), channel_id=1, source_target_pairs={{0,2},{1,65},{2,4},{3,67},{4,6},{5,69},{6,0},{7,71},{8,10},{9,73},... | collective-permute-start | bytes 393224 | tf_op jit(solution)/shard_map/ppermute | solution.py:41
  89.2 16.5 %collective-permute-start.22 = (f32[128,256]{1,0:T(8,128)S(1)}, f32[128,256]{1,0:T(8,128)S(1)}, u32[]{:S(2)}, u32[]{:S(2)}) collective-permute-start(f32[128,256]{1,0:T(8,128)S(1)} %get-tuple-element.31), channel_id=1, source_target_pairs={{0,4},{1,129},{2,6},{3,131},{4,0},{5,133},{6,2},{7,135},{8,12},{9,... | collective-permute-start | bytes 393224 | tf_op jit(solution)/shard_map/ppermute | solution.py:41
  94.1 4.3 %collective-permute-start.29 = (f32[32,256]{1,0:T(8,128)S(1)}, f32[32,256]{1,0:T(8,128)S(1)}, u32[]{:S(2)}, u32[]{:S(2)}) collective-permute-start(f32[32,256]{1,0:T(8,128)S(1)} %add_add_fusion), channel_id=1, source_target_pairs={{0,8},{1,9},{2,10},{3,11},{4,12},{5,13},{6,14},{7,15},{8,16},{9,17... | collective-permute-start | bytes 98312 | tf_op jit(solution)/shard_map/ppermute | solution.py:41
  98.4 4.4 %collective-permute-start.32 = (f32[32,256]{1,0:T(8,128)S(1)}, f32[32,256]{1,0:T(8,128)S(1)}, u32[]{:S(2)}, u32[]{:S(2)}) collective-permute-start(f32[32,256]{1,0:T(8,128)S(1)} %add.92.refs_0_), channel_id=1, source_target_pairs={{0,4},{1,129},{2,6},{3,131},{4,0},{5,133},{6,2},{7,135},{8,12},{9,... | collective-permute-start | bytes 98312 | tf_op jit(solution)/shard_map/ppermute | solution.py:41
  98.5 6.2 %collective-permute-start.31 = (f32[32,256]{1,0:T(8,128)S(1)}, f32[32,256]{1,0:T(8,128)S(1)}, u32[]{:S(2)}, u32[]{:S(2)}) collective-permute-start(f32[32,256]{1,0:T(8,128)S(1)} %add.92.refs_0_), channel_id=1, source_target_pairs={{0,2},{1,65},{2,4},{3,67},{4,6},{5,69},{6,0},{7,71},{8,10},{9,73},... | collective-permute-start | bytes 98312 | tf_op jit(solution)/shard_map/ppermute | solution.py:41
  105.7 11.6 %collective-permute-start.34 = (f32[128,256]{1,0:T(8,128)S(1)}, f32[128,256]{1,0:T(8,128)S(1)}, u32[]{:S(2)}, u32[]{:S(2)}) collective-permute-start(f32[128,256]{1,0:T(8,128)S(1)} %get-tuple-element.38.refs_0_), channel_id=1, source_target_pairs={{0,1},{1,0},{2,3},{3,2},{4,5},{5,4},{6,7},{7,6},{8,9},{9,8},{10,11... | collective-permute-start | bytes 393224 | tf_op jit(solution)/shard_map/ppermute | solution.py:41
  (14 other events, 110.3 us)
